TPU v7x, 32 devices: a whole 2x2x4 slice. The times are simulated.
32 devices in a mesh: cfg: 2 (over core), seq: 8 (over z, x), wt: 2 (over y).
Axes of the slice: x: 2, y: 2, z: 4, core: 2. Of those that a mesh axis runs over, the one named last changes fastest.
Arguments:
- hidden: bfloat16 [2, 1280, 5120], P('cfg', 'seq'), may hold values from -1.5 to 1.5
- latent: float32 [1280, 64], P('seq', 'cfg'), may hold values from -6 to 6
- tenant_lengths: int32 [4], replicated, may hold values from 1 to 960, 1280 in all
- grid_positions: int32 [1280, 3], P('seq'), may hold values from 0 to 47
- text_kv: bfloat16 [2, 2, 2048, 3072], P(None, 'cfg', None, 'wt'), may hold values from -6 to 6
- text_lengths: int32 [2, 4], P('cfg'), may hold values from 1 to 512
- w_query: bfloat16 [5120, 3072], P(('cfg', 'seq'), 'wt'), may hold values from -0.078125 to 0.078125
- w_key: bfloat16 [5120, 3072], P(('cfg', 'seq'), 'wt'), may hold values from -0.078125 to 0.078125
- w_value: bfloat16 [5120, 3072], P(('cfg', 'seq'), 'wt'), may hold values from -0.078125 to 0.078125
- w_out: bfloat16 [5120, 3072], P(('cfg', 'seq'), 'wt'), may hold values from -0.109375 to 0.109375
- w_cross_query: bfloat16 [5120, 3072], P(('cfg', 'seq'), 'wt'), may hold values from -0.078125 to 0.078125
- w_cross_out: bfloat16 [5120, 3072], P(('cfg', 'seq'), 'wt'), may hold values from -0.109375 to 0.109375
- w_head: bfloat16 [5120, 64], replicated, may hold values from -0.078125 to 0.078125
- guidance: float32 [1], replicated, may hold values from 3 to 7
- step_size: float32 [1], replicated, may hold values from -0.3 to -0.05
Outputs:
- hidden_out: bfloat16 [2, 1280, 5120], P('cfg', 'seq', 'wt')
- latent_next: float32 [1280, 64], P('seq', 'cfg')
Inputs may be any that keep to these rules, and one draw needn't show every extreme that they name: `tenant_lengths`: the lengths sum to 1280; the largest is exactly 960.
All inputs are finite; a program needn't handle non-finite values.
Results may differ from a plain program's by a relative error of at most 0.013.
Values may be sent and summed in bfloat16 or wider, within the bound.
A program may use at most 192 MiB of HBM per device.

v0:
```python
import math

import jax
import jax.numpy as jnp
from jax import lax
from jax.sharding import PartitionSpec as P

HD = 128
TEXT = 512
TENANTS = 4


epsilon = 1e-06


def partner_2(block, axis, distance):
    count = lax.axis_size(axis)
    route = []
    for low in range(count):
        high = low | 1 << distance
        if high != low and high < count:
            route += [(low, high), (high, low)]
    return lax.ppermute(block, axis, route)


def layer_norm(inputs):
    average = jnp.mean(inputs, axis=-1, keepdims=True)
    centred = inputs - average
    variance = jnp.mean(centred * centred, axis=-1, keepdims=True)
    return centred * lax.rsqrt(variance + epsilon)


def head_norm(inputs, head_dim):
    shaped = inputs.reshape(inputs.shape[:-1] + (inputs.shape[-1] // head_dim, head_dim))
    return shaped * lax.rsqrt(jnp.mean(shaped * shaped, axis=-1, keepdims=True) + epsilon)


def rotary(inputs, grid):
    head_dim = inputs.shape[-1]
    sixth_part = head_dim // 6
    angle_parts = []
    for dim_index, span_width in enumerate(
        (head_dim - 4 * sixth_part, 2 * sixth_part, 2 * sixth_part)
    ):
        exponent = jnp.arange(0, span_width, 2).astype(jnp.float32) / span_width
        frequency = 1.0 / 10000.0**exponent
        angle_parts.append(
            grid[:, dim_index : dim_index + 1].astype(jnp.float32) * frequency[None, :]
        )
    angles = jnp.concatenate(angle_parts, axis=1)[:, None, :]
    paired = inputs.reshape(inputs.shape[:-1] + (head_dim // 2, 2))
    even_part = paired[..., 0]
    odd_part = paired[..., 1]
    cosine = jnp.cos(angles)
    sinus = jnp.sin(angles)
    rotated = jnp.stack(
        [even_part * cosine - odd_part * sinus, even_part * sinus + odd_part * cosine], axis=-1
    )
    return rotated.reshape(inputs.shape)


def add_block(queries, keys, values, allowed):
    score_scale = 1.0 / math.sqrt(queries.shape[-1])
    scores = (
        jnp.einsum("qhd,khd->qhk", queries, keys, preferred_element_type=jnp.float32) * score_scale
    )
    weights = jnp.where(allowed[:, None, :], jnp.exp(scores), 0.0).astype(jnp.bfloat16)
    summed = jnp.einsum("qhk,khd->qhd", weights, values, preferred_element_type=jnp.float32)
    totals = jnp.sum(weights.astype(jnp.float32), axis=2)
    return (summed, totals)


def project_rows(normed, weight):
    return jnp.dot(
        normed,
        lax.all_gather(weight, ("cfg", "seq"), axis=0, tiled=True),
        preferred_element_type=jnp.float32,
    )


def project_out(mixed, weight):
    terms = lax.dot_general(
        mixed,
        lax.all_gather(weight, ("cfg", "seq"), axis=0, tiled=True),
        (((1,), (1,)), ((), ())),
        preferred_element_type=jnp.float32,
    )
    return lax.psum(terms.astype(jnp.bfloat16), "wt").astype(jnp.float32)


def on_device(
    hidden,
    latent,
    tenant_lengths,
    grid_positions,
    text_kv,
    text_lengths,
    w_query,
    w_key,
    w_value,
    w_out,
    w_cross_query,
    w_cross_out,
    w_head,
    guidance,
    step_size,
):
    tok_rows = hidden.shape[1]
    model_width = hidden.shape[2]
    local_cols = w_query.shape[1]
    heads_here = local_cols // HD
    seq_index = lax.axis_index("seq")
    ends = jnp.cumsum(tenant_lengths)

    def tenant_of(indices):
        return jnp.sum((indices[:, None] >= ends[None, :]).astype(jnp.int32), axis=1)

    my_tenant = tenant_of(seq_index * tok_rows + jnp.arange(tok_rows, dtype=jnp.int32))
    state = hidden[0].astype(jnp.float32)
    normed = layer_norm(state).astype(jnp.bfloat16)
    joined_weight = jnp.concatenate([w_query, w_key, w_value], axis=1)
    projected = project_rows(normed, joined_weight)
    queries = rotary(head_norm(projected[:, :local_cols], HD), grid_positions).astype(jnp.bfloat16)
    keys = rotary(head_norm(projected[:, local_cols : 2 * local_cols], HD), grid_positions).astype(
        jnp.bfloat16
    )
    keys = keys.reshape(tok_rows, local_cols)
    values = projected[:, 2 * local_cols :].astype(jnp.bfloat16)
    key_piece = lax.all_gather(keys, "seq", axis=0, tiled=True)
    value_piece = lax.all_gather(values, "seq", axis=0, tiled=True)
    piece_rows = key_piece.shape[0]
    key_tenant = tenant_of(jnp.arange(piece_rows, dtype=jnp.int32))
    allowed = my_tenant[:, None] == key_tenant[None, :]
    summed, totals = add_block(
        queries,
        key_piece.reshape(piece_rows, heads_here, HD),
        value_piece.reshape(piece_rows, heads_here, HD),
        allowed,
    )
    mixed = (summed / totals[..., None]).astype(jnp.bfloat16).reshape(tok_rows, local_cols)
    state = state + project_out(mixed, w_out)
    normed = layer_norm(state).astype(jnp.bfloat16)
    cross_queries = head_norm(project_rows(normed, w_cross_query), HD).astype(jnp.bfloat16)
    text_keys = head_norm(text_kv[0, 0].astype(jnp.float32), HD).astype(jnp.bfloat16)
    text_values = text_kv[1, 0].reshape(-1, heads_here, HD)
    text_index = jnp.arange(text_kv.shape[2], dtype=jnp.int32)
    text_tenant = text_index // TEXT
    text_slot = text_index % TEXT
    tenant_table = text_tenant[:, None] == jnp.arange(TENANTS, dtype=jnp.int32)[None, :]
    live_length = jnp.sum(jnp.where(tenant_table, text_lengths[0][None, :], 0), axis=1)
    allowed = (my_tenant[:, None] == text_tenant[None, :]) & (text_slot < live_length)[None, :]
    cross_summed, cross_totals = add_block(cross_queries, text_keys, text_values, allowed)
    cross_mixed = (
        (cross_summed / cross_totals[..., None]).astype(jnp.bfloat16).reshape(tok_rows, local_cols)
    )
    state = state + project_out(cross_mixed, w_cross_out)
    velocity = jnp.dot(
        layer_norm(state).astype(jnp.bfloat16), w_head, preferred_element_type=jnp.float32
    )
    half_index = lax.axis_index("cfg")
    channel_half = latent.shape[1]
    outgoing = lax.dynamic_slice_in_dim(velocity, (1 - half_index) * channel_half, channel_half, 1)
    partner = partner_2(outgoing, "cfg", 0)
    own_part = lax.dynamic_slice_in_dim(velocity, half_index * channel_half, channel_half, 1)
    conditional = jnp.where(half_index == 0, own_part, partner)
    null_text = jnp.where(half_index == 0, partner, own_part)
    latent_next = latent + step_size[0] * (null_text + guidance[0] * (conditional - null_text))
    slice_width = model_width // lax.axis_size("wt")
    hidden_out = lax.dynamic_slice_in_dim(
        state.astype(jnp.bfloat16), lax.axis_index("wt") * slice_width, slice_width, 1
    )
    return (hidden_out[None], latent_next)


def solution(mesh):
    return jax.shard_map(
        on_device,
        mesh=mesh,
        in_specs=(
            P("cfg", "seq", None),
            P("seq", "cfg"),
            P(),
            P("seq", None),
            P(None, "cfg", None, "wt"),
            P("cfg", None),
            P(("cfg", "seq"), "wt"),
            P(("cfg", "seq"), "wt"),
            P(("cfg", "seq"), "wt"),
            P(("cfg", "seq"), "wt"),
            P(("cfg", "seq"), "wt"),
            P(("cfg", "seq"), "wt"),
            P(),
            P(),
            P(),
        ),
        out_specs=(P("cfg", "seq", "wt"), P("seq", "cfg")),
        check_vma=False,
    )
```

profile of v0, /device:TPU:0, one launch (start us, length us, event | category | flops | bytes accessed | tf_op | source)
XLA Modules:
  0.0 949.5 jit_solution(14154485433411646982)
XLA Ops:
  7.2 3.7 pad_maximum_fusion
  12.4 233.7 %all-gather.7.cloned.1.call-done = bf16[5120,4608]{1,0:T(8,128)(2,1)} async-done(((bf16[320,4608]{1,0:T(8,128)(2,1)}), bf16[5120,4608]{1,0:T(8,128)(2,1)}) %all-gather.7.cloned.1.call-update) | async-done | bytes 47185936 | tf_op jit(solution)/shard_map/all_gather | solution.py:76
  246.1 20.1 %fusion.18 = f32[160,4608]{1,0:T(8,128)} fusion(bf16[5120,4608]{1,0:T(8,128)(2,1)} %all-gather.7.cloned.1.call-done, bf16[1,160,5120]{2,1,0:T(8,128)(2,1)S(1)} %copy-done.1, f32[160]{0:T(256)S(1)} %add_rsqrt_fusion.6, f32[160]{0:T(256)S(1)} %broadcast_multiply_fusion.7), kind=kOutput, calls=%fused_computation.31 | convolution fusion | flops 7553024000 | bytes 51774720 | tf_op jit(solution)/shard_map/dot_general | solution.py:74
  266.2 3.3 slice_multiply_fusion
  269.5 2.8 copy.72
  272.3 3.0 reshape.338
  275.3 2.8 copy.76
  278.2 3.0 reshape.340
  281.2 2.4 mul.310
  283.6 1.7 reduce_sum.140
  285.5 1.3 mul.287
  286.7 1.7 reduce_sum.139
  288.6 3.2 broadcast_multiply_fusion
  291.8 4.9 subtract_convert_fusion
  296.8 2.8 pad_maximum_fusion.1
  299.6 3.0 convert_element_type.123
  302.6 2.2 copy.74
  304.8 2.0 slice.73
  308.0 4.0 pad_maximum_fusion.2
  312.0 2.3 convert_element_type.124
  314.3 60.7 %all-gather.11.cloned.1.call-done = bf16[1280,1536]{1,0:T(8,128)(2,1)} async-done(((bf16[160,1536]{1,0:T(8,128)(2,1)}), bf16[1280,1536]{1,0:T(8,128)(2,1)}) %all-gather.11.cloned.1.call-update) | async-done | bytes 3932176 | tf_op jit(solution)/shard_map/all_gather | solution.py:129
  375.0 6.3 copy.75
  381.3 64.4 %all-gather.9.cloned.1.call-done = bf16[1280,1536]{1,0:T(8,128)(2,1)} async-done(((bf16[160,1536]{1,0:T(8,128)(2,1)}), bf16[1280,1536]{1,0:T(8,128)(2,1)}) %all-gather.9.cloned.1.call-update) | async-done | bytes 3932176 | tf_op jit(solution)/shard_map/all_gather | solution.py:130
  445.7 6.2 copy.71
  451.8 5.6 convert_reduce_fusion.1
  457.4 1.4 fusion.28
  458.9 107.6 %all-gather.13.cloned.1.call-done = bf16[5120,1536]{1,0:T(8,128)(2,1)} async-done(((bf16[320,1536]{1,0:T(8,128)(2,1)}), bf16[5120,1536]{1,0:T(8,128)(2,1)}) %all-gather.13.cloned.1.call-update) | async-done | bytes 15728656 | tf_op jit(solution)/shard_map/all_gather | solution.py:84
  566.4 11.9 %convolution_convert_fusion.1 = bf16[160,5120]{1,0:T(8,128)(2,1)} fusion(bf16[5120,1536]{1,0:T(8,128)(2,1)} %all-gather.13.cloned.1.call-done, bf16[12,20,8,128]{3,2,1,0:T(8,128)(2,1)S(1)} %fusion.28), kind=kOutput, calls=%fused_computation.13 | convolution fusion | flops 2517401600 | bytes 17858560 | tf_op jit(solution)/shard_map/dot_general | solution.py:82
  579.7 10.9 %fusion.47 = (bf16[1,1,2048,1536]{3,2,1,0:T(8,128)(2,1)}, bf16[1,1,2048,1536]{3,2,1,0:T(8,128)(2,1)}) fusion(bf16[2,1,2048,1536]{3,2,1,0:T(8,128)(2,1)} %param.19), kind=kLoop, calls=%fused_computation.109 | loop fusion | bytes 25165824 | tf_op jit(solution)/shard_map/slice | solution.py:145
  590.6 8.7 copy.95
  599.3 8.8 copy.96
  608.2 4.7 fusion.1
  613.0 1.0 compare_and_fusion
  614.0 15.6 %all-reduce.3.cloned.1.call-done = bf16[160,5120]{1,0:T(8,128)(2,1)} async-done(((bf16[160,5120]{1,0:T(8,128)(2,1)}), bf16[160,5120]{1,0:T(8,128)(2,1)}) %all-reduce.3.cloned.1.call-update) | async-done | bytes 1638416 | tf_op jit(solution)/shard_map/psum | solution.py:88
  629.6 2.1 fusion.15
  631.7 0.8 multiply_reduce_fusion.1
  632.4 119.8 %all-gather.15.cloned.1.call-done = bf16[5120,1536]{1,0:T(8,128)(2,1)} async-done(((bf16[320,1536]{1,0:T(8,128)(2,1)}), bf16[5120,1536]{1,0:T(8,128)(2,1)}) %all-gather.15.cloned.1.call-update) | async-done | bytes 15728656 | tf_op jit(solution)/shard_map/all_gather | solution.py:76
  752.3 7.6 fusion.16
  759.8 1.2 reshape.342
  761.1 1.9 multiply_reduce_fusion.2
  763.2 1.9 multiply_convert_fusion.4
  765.0 7.7 convert_reduce_fusion
  772.8 2.2 fusion.29
  775.0 98.2 %all-gather.17.cloned.1.call-done = bf16[5120,1536]{1,0:T(8,128)(2,1)} async-done(((bf16[320,1536]{1,0:T(8,128)(2,1)}), bf16[5120,1536]{1,0:T(8,128)(2,1)}) %all-gather.17.cloned.1.call-update) | async-done | bytes 15728656 | tf_op jit(solution)/shard_map/all_gather | solution.py:84
  873.2 11.9 %convolution_convert_fusion = bf16[160,5120]{1,0:T(8,128)(2,1)} fusion(bf16[5120,1536]{1,0:T(8,128)(2,1)} %all-gather.17.cloned.1.call-done, bf16[12,20,8,128]{3,2,1,0:T(8,128)(2,1)S(1)} %fusion.29), kind=kOutput, calls=%fused_computation.12 | convolution fusion | flops 2517401600 | bytes 17858560 | tf_op jit(solution)/shard_map/dot_general | solution.py:82
  886.4 49.9 %all-reduce.5.cloned.1.call-done = bf16[160,5120]{1,0:T(8,128)(2,1)} async-done(((bf16[160,5120]{1,0:T(8,128)(2,1)}), bf16[160,5120]{1,0:T(8,128)(2,1)}) %all-reduce.5.cloned.1.call-update) | async-done | bytes 1638416 | tf_op jit(solution)/shard_map/psum | solution.py:88
  936.4 2.6 fusion.46
  940.4 1.0 fusion.30
  (75 shorter events, 6.7 us)
Async XLA Ops:
  7.2 932.4 %copy-start = (bf16[5120,64]{0,1:T(8,128)(2,1)S(1)}, bf16[5120,64]{0,1:T(8,128)(2,1)}, u32[]{:S(2)}) copy-start(bf16[5120,64]{0,1:T(8,128)(2,1)} %param.27) | copy-start | bytes 1966084
  7.2 3.9 copy-start.6
  7.2 4.3 copy-start.1
  7.2 238.9 %all-gather.7.cloned.1.call-start = ((), (), s32[]{:S(2)}) async-start(), calls=%async_computation | async-start | bytes 50135040 | tf_op jit(solution)/shard_map/all_gather | solution.py:76
  11.0 364.0 %all-gather.11.cloned.1.call-start = ((), (), s32[]{:S(2)}) async-start(), calls=%async_computation.2 | async-start | bytes 4423680 | tf_op jit(solution)/shard_map/all_gather | solution.py:129
  299.6 7.9 copy-start.8
  304.7 140.9 %all-gather.9.cloned.1.call-start = ((), (), s32[]{:S(2)}) async-start(), calls=%async_computation.1 | async-start | bytes 4423680 | tf_op jit(solution)/shard_map/all_gather | solution.py:130
  306.8 259.6 %all-gather.13.cloned.1.call-start = ((), (), s32[]{:S(2)}) async-start(), calls=%async_computation.3 | async-start | bytes 16711680 | tf_op jit(solution)/shard_map/all_gather | solution.py:84
  307.4 322.2 %all-reduce.3.cloned.1.call-start = ((), (), s32[]{:S(2)}) async-start(), calls=%async_computation.4 | async-start | bytes 3276800 | tf_op jit(solution)/shard_map/psum | solution.py:88
  451.8 5.6 copy-start.3
  578.3 173.9 %all-gather.15.cloned.1.call-start = ((), (), s32[]{:S(2)}) async-start(), calls=%async_computation.5 | async-start | bytes 16711680 | tf_op jit(solution)/shard_map/all_gather | solution.py:76
  578.9 294.3 %all-gather.17.cloned.1.call-start = ((), (), s32[]{:S(2)}) async-start(), calls=%async_computation.6 | async-start | bytes 16711680 | tf_op jit(solution)/shard_map/all_gather | solution.py:84
  579.7 356.7 %all-reduce.5.cloned.1.call-start = ((), (), s32[]{:S(2)}) async-start(), calls=%async_computation.7 | async-start | bytes 3276800 | tf_op jit(solution)/shard_map/psum | solution.py:88
  599.3 8.8 copy-start.7
  629.6 2.1 copy-start.2
  761.1 4.0 copy-start.4
  763.1 9.6 %slice-start = ((s8[6291456]{0:T(1024)(128)(4,1)}), s8[4194304]{0:T(1024)(128)(4,1)S(1)}, s32[]{:S(2)}) async-start(s8[6291456]{0:T(1024)(128)(4,1)} %bitcast.95), calls=%async_computation.8 | async-start | bytes 8388608
  765.0 7.8 slice-start.1
  939.5 2.1 copy-start.5
  940.3 1.3 collective-permute-start
Sparse Core Ops, SparseCore 0:
  11.1 234.9 all-gather.6
  304.9 70.0 all-gather.10
  377.2 68.4 all-gather.8
  447.7 118.6 all-gather.12
  578.5 51.0 all-reduce.2
  631.9 120.2 all-gather.14
  754.7 118.4 all-gather.16
  885.2 51.0 all-reduce.4
where the time goes:
time: 959 us; the launch traced here: 949 us
  waiting for transfers between devices  752 us (78%)
  matrix products  69 us (7%)
  local copies, waits for them, and re-layouts  68.3 us (7%)
  other arithmetic  43.5 us (5%)
  between operations  16.2 us (2%)
    all_gather x2, waiting for transfers between devices, project_rows(): lax.all_gather(weight, ('cfg', 'seq'), axis=0, tiled=True)  354 us
    all_gather x2, waiting for transfers between devices, project_out(): lax.all_gather(weight, ('cfg', 'seq'), axis=0, tiled=True)  206 us
    psum x2, waiting for transfers between devices, project_out(): return lax.psum(terms.astype(jnp.bfloat16), 'wt').astype(jnp.float32)  65.5 us
    all_gather x1, waiting for transfers between devices, on_device(): value_piece = lax.all_gather(values, 'seq', axis=0, tiled=True)  64.4 us
    all_gather x1, waiting for transfers between devices, on_device(): key_piece = lax.all_gather(keys, 'seq', axis=0, tiled=True)  60.7 us
    dot_general x2, matrix products, project_rows(): jnp.dot(normed, lax.all_gather(weight, ('cfg', 'seq'), axis=0, tiled=True...  27.6 us
    dot_general x2, matrix products, project_out(): lax.dot_general(mixed, lax.all_gather(weight, ('cfg', 'seq'), axis=0, til...  23.7 us
  transfers between devices with their start and end apart: 9, of which 9 were waited for; matrix products, arithmetic and copies ran while one was open for 10% of the time, Pallas kernels for 0%

commit v1 on v0

v1 whole, which is shorter than its diff:
```python
import math

import jax
import jax.numpy as jnp
import numpy as np
from jax import lax
from jax.sharding import Mesh
from jax.sharding import PartitionSpec as P

HD = 128
TEXT = 512
TENANTS = 4
EPS = 1e-06
BF = jnp.bfloat16
F32 = jnp.float32


def flip(block, axis):
    return lax.ppermute(block, axis, [(0, 1), (1, 0)])


def rotary_tables():
    sixth = HD // 6
    table = np.zeros((3, HD), np.float32)
    lane = 0
    for column, span in enumerate((HD - 4 * sixth, 2 * sixth, 2 * sixth)):
        exponent = np.arange(0, span, 2).astype(np.float32) / np.float32(span)
        frequency = (1.0 / 10000.0**exponent).astype(np.float32)
        table[column, lane : lane + span] = np.repeat(frequency, 2)
        lane += span
    swap = np.zeros((HD, HD), np.float32)
    for pair in range(0, HD, 2):
        swap[pair + 1, pair] = -1.0
        swap[pair, pair + 1] = 1.0
    return table, swap


def head_scale(shaped):
    return lax.rsqrt(jnp.mean(shaped * shaped, axis=-1, keepdims=True) + EPS)


def attend(queries, keys, values, allowed):
    scores = jnp.einsum("qhd,khd->hqk", queries, keys, preferred_element_type=F32)
    scores = scores * (1.0 / math.sqrt(queries.shape[-1]))
    weights = jnp.where(allowed[None], jnp.exp(scores), 0.0).astype(BF)
    summed = jnp.einsum("hqk,khd->qhd", weights, values, preferred_element_type=F32)
    totals = jnp.sum(weights.astype(F32), axis=2).T
    return (summed / totals[..., None]).astype(BF).reshape(queries.shape[0], -1)


def on_device(
    hidden,
    latent,
    tenant_lengths,
    grid_positions,
    text_kv,
    text_lengths,
    w_query,
    w_key,
    w_value,
    w_out,
    w_cross_query,
    w_cross_out,
    w_head,
    guidance,
    step_size,
):
    halves, groups, parts, columns = (lax.axis_size(a) for a in ("cfg", "z", "t", "wt"))
    half_index, z_index, t_index, wt_index = (
        lax.axis_index(a) for a in ("cfg", "z", "t", "wt")
    )
    tok, width = hidden.shape[1:]
    rows = groups * tok
    local_cols = w_query.shape[1]
    my_cols = local_cols // groups
    heads = my_cols // HD
    paired = halves == 2 and parts == 2
    block = w_query.shape[0]
    ends = jnp.cumsum(tenant_lengths)

    def tenant_of(indices):
        return jnp.sum((indices[:, None] >= ends[None, :]).astype(jnp.int32), axis=1)

    def wide(w):
        if not paired:
            return lax.all_gather(w, ("cfg", "t"), axis=0, tiled=True)
        two = jnp.concatenate([w, flip(w, "t")], axis=0)
        return jnp.concatenate([two, flip(two, "cfg")], axis=0)

    def local_order(x):
        if not paired:
            return x
        x = jnp.where(t_index == 1, x[..., ::-1, :], x)
        return jnp.where(half_index == 1, x[..., ::-1, :, :], x)

    def over_groups(x):
        return x if groups == 1 else lax.all_to_all(x, "z", 0, 0, tiled=True)

    def join_groups(x):
        if groups == 1:
            return x
        x = lax.all_gather(x, "z", axis=0)
        return jnp.swapaxes(x, 0, 1).reshape(rows, local_cols)

    def sum_groups(x):
        if groups == 1:
            return x
        return lax.psum_scatter(x, "z", scatter_dimension=0, tiled=True)

    def to_groups(x, n):
        return jnp.swapaxes(x.reshape(x.shape[0], groups, n), 0, 1)

    def both_columns(terms):
        terms = terms.astype(BF)
        if columns == 1:
            return terms.astype(F32)
        if columns == 2:
            return terms.astype(F32) + flip(terms, "wt").astype(F32)
        return lax.psum(terms, "wt").astype(F32)

    wide_query, wide_key, wide_value = wide(w_query), wide(w_key), wide(w_value)
    wide_out, wide_cross, wide_cross_out = wide(w_out), wide(w_cross_query), wide(w_cross_out)

    own = hidden[0]
    sliced = local_order(
        jnp.transpose(own.reshape(tok, halves, groups, parts, block), (2, 0, 1, 3, 4))
    ).reshape(rows, width // groups)
    sliced = over_groups(sliced).astype(F32)
    own = own.astype(F32)
    mean = jnp.mean(own, axis=-1, keepdims=True)
    centred = own - mean
    scale = lax.rsqrt(jnp.mean(centred * centred, axis=-1, keepdims=True) + EPS)
    facts = jnp.concatenate([mean, scale, grid_positions.astype(F32)], axis=1)
    if groups > 1:
        facts = lax.all_gather(facts, "z", axis=0, tiled=True)
    normed = ((sliced - facts[:, 0:1]) * facts[:, 1:2]).astype(BF)

    projected = jnp.concatenate(
        [
            to_groups(jnp.dot(normed, w, preferred_element_type=F32).astype(BF), my_cols)
            for w in (wide_query, wide_key, wide_value)
        ],
        axis=2,
    )
    projected = sum_groups(projected.reshape(groups * rows, 3 * my_cols))

    table, swap = rotary_tables()
    angles = (
        facts[:, 2:3] * table[0][None] + facts[:, 3:4] * table[1][None] + facts[:, 4:5] * table[2][None]
    )
    cosine, sinus = jnp.cos(angles)[:, None, :], jnp.sin(angles)[:, None, :]

    def rotated(x):
        shaped = x.reshape(rows, heads, HD)
        swapped = jnp.einsum("thd,de->the", shaped, jnp.asarray(swap, BF), preferred_element_type=F32)
        shaped = shaped.astype(F32)
        return ((shaped * cosine + swapped * sinus) * head_scale(shaped)).astype(BF)

    queries = rotated(projected[:, :my_cols])
    keys = rotated(projected[:, my_cols : 2 * my_cols]).reshape(rows, my_cols)
    key_value = jnp.concatenate([keys, projected[:, 2 * my_cols :]], axis=1)

    base = (jnp.arange(groups, dtype=jnp.int32) * parts * tok)[:, None] + jnp.arange(
        tok, dtype=jnp.int32
    )[None]
    base = base.reshape(-1)
    my_tenant = tenant_of(base + t_index * tok)
    if parts == 2:
        key_value = jnp.concatenate([key_value, flip(key_value, "t")], axis=0)
        key_tenant = jnp.concatenate([my_tenant, tenant_of(base + (1 - t_index) * tok)])
    else:
        key_value = lax.all_gather(key_value, "t", axis=0, tiled=True)
        key_tenant = tenant_of(
            (jnp.arange(parts, dtype=jnp.int32)[:, None] * tok + base[None]).reshape(-1)
        )
    mixed = attend(
        queries,
        key_value[:, :my_cols].reshape(-1, heads, HD),
        key_value[:, my_cols:].reshape(-1, heads, HD),
        my_tenant[:, None] == key_tenant[None, :],
    )

    def project_out(mixed, weight):
        return lax.dot_general(
            join_groups(mixed), weight, (((1,), (1,)), ((), ())), preferred_element_type=F32
        )

    state = sliced + both_columns(project_out(mixed, wide_out))

    shifted = state - facts[:, 0:1]
    sums = jnp.concatenate(
        [jnp.sum(shifted, axis=1, keepdims=True), jnp.sum(shifted * shifted, axis=1, keepdims=True)],
        axis=1,
    )
    if groups > 1:
        sums = lax.psum(sums, "z")
    sums = sums / width
    scale = lax.rsqrt(jnp.maximum(sums[:, 1:2] - sums[:, 0:1] ** 2, 0.0) + EPS)
    normed = ((shifted - sums[:, 0:1]) * scale).astype(BF)
    crossed = jnp.dot(normed, wide_cross, preferred_element_type=F32).astype(BF)
    crossed = to_groups(crossed, my_cols).reshape(groups, rows, my_cols)
    crossed = jnp.sum(
        over_groups(crossed.reshape(groups * rows, my_cols))
        .reshape(groups, rows, my_cols)
        .astype(F32),
        axis=0,
    )
    shaped = crossed.reshape(rows, heads, HD)
    cross_queries = (shaped * head_scale(shaped)).astype(BF)
    text = lax.dynamic_slice_in_dim(text_kv[:, 0], z_index * my_cols, my_cols, 2)
    text_keys = text[0].reshape(-1, heads, HD).astype(F32)
    text_keys = (text_keys * head_scale(text_keys)).astype(BF)
    text_values = text[1].reshape(-1, heads, HD)
    text_index = jnp.arange(text_kv.shape[2], dtype=jnp.int32)
    text_tenant = text_index // TEXT
    table = text_tenant[:, None] == jnp.arange(TENANTS, dtype=jnp.int32)[None, :]
    live_length = jnp.sum(jnp.where(table, text_lengths[0][None, :], 0), axis=1)
    allowed = (my_tenant[:, None] == text_tenant[None, :]) & (text_index % TEXT < live_length)[None]
    cross_mixed = attend(cross_queries, text_keys, text_values, allowed)
    terms = project_out(cross_mixed, wide_cross_out)

    head_rows = w_head.reshape(halves, groups, parts, block, -1)
    head_rows = lax.dynamic_index_in_dim(head_rows, z_index, 1, keepdims=False)
    if paired:
        head_rows = jnp.where(t_index == 1, head_rows[:, ::-1], head_rows)
        head_rows = jnp.where(half_index == 1, head_rows[::-1], head_rows)
    channels = head_rows.shape[-1]
    head_rows = head_rows.reshape(-1, channels)

    final = state + both_columns(terms)
    out_width = width // columns
    if groups == 1:
        hidden_out = lax.dynamic_slice_in_dim(final.astype(BF), wt_index * out_width, out_width, 1)
    else:
        leaving = final.astype(BF).reshape(groups, tok, halves, parts, block)
        if paired:
            leaving = jnp.where(t_index == 1, leaving[:, :, :, ::-1], leaving)
            leaving = jnp.where(half_index == 1, leaving[:, :, ::-1], leaving)
        if columns == halves:
            leaving = lax.dynamic_index_in_dim(leaving, wt_index, 2, keepdims=True)
        leaving = over_groups(leaving)
        hidden_out = jnp.transpose(leaving, (1, 2, 0, 3, 4)).reshape(tok, -1)
        if columns != halves:
            hidden_out = lax.dynamic_slice_in_dim(hidden_out, wt_index * out_width, out_width, 1)

    shifted = final - facts[:, 0:1]
    sums = jnp.concatenate(
        [
            jnp.dot(shifted.astype(BF), head_rows, preferred_element_type=F32),
            jnp.sum(shifted, axis=1, keepdims=True),
            jnp.sum(shifted * shifted, axis=1, keepdims=True),
        ],
        axis=1,
    )
    if groups > 1:
        sums = jnp.sum(over_groups(sums).reshape(groups, tok, -1), axis=0)
    mean = sums[:, channels : channels + 1] / width
    square = sums[:, channels + 1 :] / width
    scale = lax.rsqrt(jnp.maximum(square - mean * mean, 0.0) + EPS)
    totals = jnp.sum(w_head.astype(F32), axis=0)[None]
    velocity = (sums[:, :channels] - mean * totals) * scale

    channel_half = latent.shape[1]
    outgoing = lax.dynamic_slice_in_dim(velocity, (1 - half_index) * channel_half, channel_half, 1)
    partner = flip(outgoing, "cfg")
    own_part = lax.dynamic_slice_in_dim(velocity, half_index * channel_half, channel_half, 1)
    conditional = jnp.where(half_index == 0, own_part, partner)
    null_text = jnp.where(half_index == 0, partner, own_part)
    latent_next = latent + step_size[0] * (null_text + guidance[0] * (conditional - null_text))
    return (hidden_out[None], latent_next)


def solution(mesh):
    halves, seq, columns = (mesh.shape[a] for a in ("cfg", "seq", "wt"))

    def run(*args):
        heads_here = args[6].shape[1] // columns // HD
        groups = math.gcd(heads_here, seq)
        fine = Mesh(
            mesh.devices.reshape(halves, groups, seq // groups, columns), ("cfg", "z", "t", "wt")
        )
        seq_axes = ("z", "t")
        weight = P(("cfg", "z", "t"), "wt")
        return jax.shard_map(
            on_device,
            mesh=fine,
            in_specs=(
                P("cfg", seq_axes, None),
                P(seq_axes, "cfg"),
                P(),
                P(seq_axes, None),
                P(None, "cfg", None, "wt"),
                P("cfg", None),
                weight,
                weight,
                weight,
                weight,
                weight,
                weight,
                P(),
                P(),
                P(),
            ),
            out_specs=(P("cfg", seq_axes, "wt"), P(seq_axes, "cfg")),
            check_vma=False,
        )(*args)

    return run
```

time: 959 us -> 629 us (0.66)
  waiting for transfers between devices: 752 us -> 333 us
  blocking collectives: 0 us -> 34.1 us
  starting transfers between devices: 0.39 us -> 31.7 us
  local copies, waits for them, and re-layouts: 68.3 us -> 97.8 us
  matrix products: 69 us -> 54.6 us
  other arithmetic: 43.5 us -> 54.2 us
    all_gather x6 -> x2, waiting for transfers between devices: 684 us -> 80.6 us  [join_groups(): x = lax.all_gather(x, 'z', axis=0)]
    reduce_scatter x0 -> x1, waiting for transfers between devices: none -> 102 us  [sum_groups(): return lax.psum_scatter(x, 'z', scatter_dimension=0, tiled=True)]
    ppermute x1 -> x16, waiting for transfers between devices: 0.21 us -> 98.7 us  [flip(): return lax.ppermute(block, axis, [(0, 1), (1, 0)])]
    psum x2 -> x0, waiting for transfers between devices: 65.5 us -> none  [project_out(): return lax.psum(terms.astype(jnp.bfloat16), 'wt').astype(jnp.float32)]
    all_to_all x0 -> x4, waiting for transfers between devices: none -> 52.2 us  [over_groups(): return x if groups == 1 else lax.all_to_all(x, 'z', 0, 0, tiled=True)]
    rev x0 -> x4, local copies, waits for them, and re-layouts: none -> 38.6 us  [the longest x1 18.2 us: local_order(): x = jnp.where(t_index == 1, x[..., ::-1, :], x)]
    all_gather x0 -> x1, blocking collectives: none -> 24 us  [on_device(): facts = lax.all_gather(facts, 'z', axis=0, tiled=True)]
    concatenate x1 -> x12, other arithmetic: 3.72 us -> 20.9 us  [the longest x6 14.7 us: wide(): two = jnp.concatenate([w, flip(w, 't')], axis=0)]
  transfers between devices with their start and end apart: 9 -> 23, of which waited for: 9 -> 9; matrix products, arithmetic and copies ran while one was open for 10% -> 24% of each run, Pallas kernels for 0% -> 0%
where the time goes in v1:
time: 629 us; the launch traced here: 621 us
  waiting for transfers between devices  333 us (53%)
  local copies, waits for them, and re-layouts  97.8 us (16%)
  matrix products  54.6 us (9%)
  other arithmetic  54.2 us (9%)
  blocking collectives  34.1 us (5%)
  starting transfers between devices  31.7 us (5%)
  between operations  15.8 us (3%)
    reduce_scatter x1, waiting for transfers between devices, sum_groups(): return lax.psum_scatter(x, 'z', scatter_dimension=0, tiled=True)  102 us
    ppermute x16, waiting for transfers between devices, flip(): return lax.ppermute(block, axis, [(0, 1), (1, 0)])  98.7 us
    all_gather x2, waiting for transfers between devices, join_groups(): x = lax.all_gather(x, 'z', axis=0)  80.6 us
    all_to_all x4, waiting for transfers between devices, over_groups(): return x if groups == 1 else lax.all_to_all(x, 'z', 0, 0, tiled=True)  52.2 us
    all_gather x1, blocking collectives, on_device(): facts = lax.all_gather(facts, 'z', axis=0, tiled=True)  24 us
    rev x1, local copies, waits for them, and re-layouts, local_order(): x = jnp.where(t_index == 1, x[..., ::-1, :], x)  18.2 us
    all_to_all x4, starting transfers between devices, over_groups(): return x if groups == 1 else lax.all_to_all(x, 'z', 0, 0, tiled=True)  17 us
    concatenate x6, other arithmetic, wide(): two = jnp.concatenate([w, flip(w, 't')], axis=0)  14.7 us
  transfers between devices with their start and end apart: 23, of which 9 were waited for; matrix products, arithmetic and copies ran while one was open for 24% of the time, Pallas kernels for 0%

profile of v1, /device:TPU:0, one launch (start us, length us, event | category | flops | bytes accessed | tf_op | source)
XLA Modules:
  0.0 621.3 jit_solution(4115814214780540290)
XLA Ops:
  7.2 3.0 collective-permute-start
  10.2 5.2 reshape_squeeze.7
  15.4 2.6 copy.149
  18.0 18.2 %rev.18 = bf16[4,160,2,2,320]{4,3,2,1,0:T(2,128)(2,1)} reverse(bf16[4,160,2,2,320]{4,3,2,1,0:T(2,128)(2,1)} %bitcast.122), dimensions={3} | reverse | bytes 3276800 | tf_op jit(solution)/shard_map/rev | solution.py:93
  38.3 3.3 broadcast_select_fusion.2
  41.6 5.5 all_to_all.17
  47.1 4.9 all-to-all-start
  54.4 3.0 pad_maximum_fusion.1
  58.0 18.9 %collective-permute-done.4 = bf16[320,1536]{1,0:T(8,128)(2,1)S(1)} collective-permute-done((bf16[320,1536]{1,0:T(8,128)(2,1)}, bf16[320,1536]{1,0:T(8,128)(2,1)S(1)}, u32[]{:S(2)}, u32[]{:S(2)}) %collective-permute-start.4) | collective-permute-done | bytes 983072 | tf_op jit(solution)/shard_map/ppermute | solution.py:19
  78.6 24.0 %all-gather = f32[4,160,5]{1,2,0:T(8,128)S(1)} all-gather(f32[1,160,5]{1,2,0:T(8,128)S(1)} %maximum_bitcast_fusion), channel_id=1, replica_groups=mesh['cfg'=2,'z'=4,'t'=2,'wt'=2] {'z'}, dimensions={0}, use_global_device_ids=true | all-gather | bytes 16000 | tf_op jit(solution)/shard_map/all_gather | solution.py:135
  102.7 3.0 pad_maximum_fusion.2
  106.3 4.5 fusion.56
  112.3 4.2 fusion.50
  116.5 4.5 fusion.53
  121.5 3.0 pad_maximum_fusion
  129.2 101.5 %reduce-scatter.2.cloned.1.call-done = bf16[640,1152]{1,0:T(8,128)(2,1)} async-done(((bf16[2560,1152]{1,0:T(8,128)(2,1)}), bf16[640,1152]{1,0:T(8,128)(2,1)}) %reduce-scatter.2.cloned.1.call-update) | async-done | bytes 1474576 | tf_op jit(solution)/shard_map/reduce_scatter | solution.py:108
  243.9 18.7 %collective-permute-done.6 = bf16[640,768]{1,0:T(8,128)(2,1)} collective-permute-done((bf16[640,768]{1,0:T(8,128)(2,1)}, bf16[640,768]{1,0:T(8,128)(2,1)}, u32[]{:S(2)}, u32[]{:S(2)}) %collective-permute-start.6) | collective-permute-done | bytes 983072 | tf_op jit(solution)/shard_map/ppermute | solution.py:19
  265.1 2.3 copy.104
  268.8 6.9 %convert_reduce_fusion.1 = (f32[3,640]{1,0:T(4,128)S(1)}, bf16[3,640,1280]{2,1,0:T(8,128)(2,1)}) fusion(bf16[1280,3,128]{0,2,1:T(8,128)(2,1)} %bitcast.142, bf16[128,128,1]{0,1,2:T(8,128)(2,1)S(1)} %copy-done.15, bf16[640,3,128]{0,2,1:T(8,128)(2,1)S(1)} %bitcast.136, f32[640,3]{0,1:T(4,128)S(1)} %add_rsqrt_fusion.2, f32[640,128]{0,1:T(8,128)} %get-tuple-element.29, ...), kind=kOutput, calls=%fused_computation.2 | convolution fusion | flops 705820800 | bytes 7912448 | tf_op jit(solution)/shard_map/qhd,khd->hqk/dot_general | solution.py:43
  275.6 3.9 fusion.73
  280.6 2.9 pad_maximum_fusion.5
  285.0 39.8 %all-gather.4.cloned.1.call-done = bf16[4,640,384]{2,1,0:T(8,128)(2,1)} async-done(((bf16[1,640,384]{2,1,0:T(8,128)(2,1)}), bf16[4,640,384]{2,1,0:T(8,128)(2,1)}) %all-gather.4.cloned.1.call-update) | async-done | bytes 1966096 | tf_op jit(solution)/shard_map/all_gather | solution.py:102
  324.9 4.2 copy.113
  329.0 5.4 fusion.47
  336.0 2.6 pad_maximum_fusion.6
  338.7 33.4 %collective-permute-done.9 = bf16[640,1280]{1,0:T(8,128)(2,1)S(1)} collective-permute-done((bf16[640,1280]{1,0:T(8,128)(2,1)S(1)}, bf16[640,1280]{1,0:T(8,128)(2,1)S(1)}, u32[]{:S(2)}, u32[]{:S(2)}) %collective-permute-start.9) | collective-permute-done | bytes 1638432 | tf_op jit(solution)/shard_map/ppermute | solution.py:19
  372.1 2.5 subtract_reduce_fusion.1
  374.6 10.1 %psum.7 = f32[640,2]{0,1:T(2,128)S(1)} all-reduce(f32[640,2]{0,1:T(2,128)S(1)} %pad_maximum_fusion.10), channel_id=1, replica_groups=mesh['cfg'=2,'z'=4,'t'=2,'wt'=2] {'z'}, use_global_device_ids=true, to_apply=%region_12.13 | all-reduce | flops 1280 | bytes 10240 | tf_op jit(solution)/shard_map/psum | solution.py:196
  384.8 5.6 fusion.44
  391.9 3.6 all-to-all-start.1
  396.8 3.4 constant_dynamic-slice_fusion.2
  407.1 31.4 %all-to-all-done.1 = bf16[4,640,384]{2,1,0:T(8,128)(2,1)S(1)} async-done(((bf16[4,640,384]{2,1,0:T(8,128)(2,1)}), bf16[4,640,384]{2,1,0:T(8,128)(2,1)S(1)}, u32[]{:S(2)}, u32[]{:S(2)}) %all-to-all-start.1) | async-done | bytes 1966112 | tf_op jit(solution)/shard_map/all_to_all | solution.py:97
  441.4 6.2 convert_reduce_fusion
  447.7 2.5 fusion.75
  452.9 40.8 %all-gather.6.cloned.1.call-done = bf16[4,640,384]{2,1,0:T(8,128)(2,1)} async-done(((bf16[1,640,384]{2,1,0:T(8,128)(2,1)}), bf16[4,640,384]{2,1,0:T(8,128)(2,1)}) %all-gather.6.cloned.1.call-update) | async-done | bytes 1966096 | tf_op jit(solution)/shard_map/all_gather | solution.py:102
  493.7 4.0 copy.121
  497.7 6.7 %fusion.41 = bf16[640,1280]{1,0:T(8,128)(2,1)} fusion(bf16[640,1536]{0,1:T(8,128)(2,1)} %bitcast.132, bf16[640,1536]{1,0:T(8,128)(2,1)} %collective-permute-done.13, bf16[320,1536]{1,0:T(8,128)(2,1)} %collective-permute-done.12, bf16[320,1536]{1,0:T(8,128)(2,1)} %param.31), kind=kOutput, calls=%fused_computation.61 | convolution fusion | flops 2529198080 | bytes 7536640 | tf_op jit(solution)/shard_map/dot_general | solution.py:184
  505.9 3.6 reshape.472
  514.6 27.6 %collective-permute-done.14 = bf16[640,1280]{1,0:T(8,128)(2,1)} collective-permute-done((bf16[640,1280]{1,0:T(8,128)(2,1)}, bf16[640,1280]{1,0:T(8,128)(2,1)}, u32[]{:S(2)}, u32[]{:S(2)}) %collective-permute-start.14) | collective-permute-done | bytes 1638432 | tf_op jit(solution)/shard_map/ppermute | solution.py:19
  542.2 3.8 subtract_convert_fusion
  547.9 4.6 reshape.471
  552.5 14.2 %rev.20 = bf16[4,160,2,2,320]{4,3,2,1,0:T(2,128)(2,1)} reverse(bf16[4,160,2,2,320]{4,3,2,1,0:T(2,128)(2,1)S(1)} %reshape.471), dimensions={3} | reverse | bytes 3276800 | tf_op jit(solution)/shard_map/rev | solution.py:237
  569.7 3.5 all-to-all-start.3
  573.2 3.3 broadcast_select_fusion
  576.5 4.3 rev.21
  580.8 3.2 broadcast_select_fusion.3
  584.0 5.0 all-to-all-start.2
  591.4 20.8 %all-to-all-done.2 = bf16[4,160,1,2,320]{4,3,2,1,0:T(2,128)(2,1)S(1)} async-done(((bf16[4,160,1,2,320]{4,3,2,1,0:T(2,128)(2,1)}), bf16[4,160,1,2,320]{4,3,2,1,0:T(2,128)(2,1)S(1)}, u32[]{:S(2)}, u32[]{:S(2)}) %all-to-all-start.2) | async-done | bytes 819232 | tf_op jit(solution)/shard_map/all_to_all | solution.py:97
  (156 shorter events, 65.4 us)
Async XLA Ops:
  7.2 47.3 %collective-permute-start = (bf16[320,1536]{1,0:T(8,128)(2,1)}, bf16[320,1536]{1,0:T(8,128)(2,1)}, u32[]{:S(2)}, u32[]{:S(2)}) collective-permute-start(bf16[320,1536]{1,0:T(8,128)(2,1)} %param.26), channel_id=1, source_target_pairs={{0,2},{2,0},{1,3},{3,1},{4,6},{6,4},{5,7},{7,5},{8,10},{10,8},{9,1... | collective-permute-start | bytes 2949128 | tf_op jit(solution)/shard_map/ppermute | solution.py:19
  41.6 12.5 %copy-start.17 = (s32[160,3]{0,1:T(4,128)S(1)}, s32[160,3]{0,1:T(4,128)}, u32[]{:S(2)}) copy-start(s32[160,3]{0,1:T(4,128)} %param.23) | copy-start | bytes 5764
  41.6 12.5 %copy-start = (bf16[1,160,5120]{2,1,0:T(8,128)(2,1)S(1)}, bf16[1,160,5120]{2,1,0:T(8,128)(2,1)}, u32[]{:S(2)}) copy-start(bf16[1,160,5120]{2,1,0:T(8,128)(2,1)} %param.20) | copy-start | bytes 4915204
  47.1 58.7 %all-to-all-start = ((bf16[4,160,1280]{2,1,0:T(8,128)(2,1)}), bf16[4,160,1280]{2,1,0:T(8,128)(2,1)S(1)}, u32[]{:S(2)}, u32[]{:S(2)}) async-start(bf16[4,160,1280]{2,1,0:T(8,128)(2,1)} %all_to_all.17), calls=%async_computation | async-start | bytes 3276800 | tf_op jit(solution)/shard_map/all_to_all | solution.py:97
  51.9 178.7 %reduce-scatter.2.cloned.1.call-start = ((), (), s32[]{:S(2)}) async-start(), calls=%async_computation.5 | async-start | bytes 7372800 | tf_op jit(solution)/shard_map/reduce_scatter | solution.py:108
  51.9 24.9 %collective-permute-start.4 = (bf16[320,1536]{1,0:T(8,128)(2,1)}, bf16[320,1536]{1,0:T(8,128)(2,1)S(1)}, u32[]{:S(2)}, u32[]{:S(2)}) collective-permute-start(bf16[320,1536]{1,0:T(8,128)(2,1)} %param.28), channel_id=1, source_target_pairs={{0,2},{2,0},{1,3},{3,1},{4,6},{6,4},{5,7},{7,5},{8,10},{10,8},{9,1... | collective-permute-start | bytes 2949128 | tf_op jit(solution)/shard_map/ppermute | solution.py:19
  54.0 48.7 %collective-permute-start.2 = (bf16[320,1536]{1,0:T(8,128)(2,1)}, bf16[320,1536]{1,0:T(8,128)(2,1)}, u32[]{:S(2)}, u32[]{:S(2)}) collective-permute-start(bf16[320,1536]{1,0:T(8,128)(2,1)} %param.27), channel_id=1, source_target_pairs={{0,2},{2,0},{1,3},{3,1},{4,6},{6,4},{5,7},{7,5},{8,10},{10,8},{9,1... | collective-permute-start | bytes 2949128 | tf_op jit(solution)/shard_map/ppermute | solution.py:19
  54.4 22.5 %copy-start.8 = (bf16[320,1536]{1,0:T(8,128)(2,1)S(1)}, bf16[320,1536]{1,0:T(8,128)(2,1)}, u32[]{:S(2)}) copy-start(bf16[320,1536]{1,0:T(8,128)(2,1)} %param.28) | copy-start | bytes 2949124
  57.4 48.8 %collective-permute-start.1 = (bf16[640,1536]{1,0:T(8,128)(2,1)}, bf16[640,1536]{1,0:T(8,128)(2,1)}, u32[]{:S(2)}, u32[]{:S(2)}) collective-permute-start(bf16[640,1536]{1,0:T(8,128)(2,1)} %pad_maximum_fusion.1), channel_id=1, source_target_pairs={{0,16},{16,0},{1,17},{17,1},{2,18},{18,2},{3,19},{19,3},{4,20},{20... | collective-permute-start | bytes 5898248 | tf_op jit(solution)/shard_map/ppermute | solution.py:19
  76.9 1.7 copy-start.12
  78.6 32.4 %collective-permute-start.5 = (bf16[640,1536]{1,0:T(8,128)(2,1)}, bf16[640,1536]{1,0:T(8,128)(2,1)}, u32[]{:S(2)}, u32[]{:S(2)}) collective-permute-start(bf16[640,1536]{1,0:T(8,128)(2,1)} %pad_maximum_fusion.3), channel_id=1, source_target_pairs={{0,16},{16,0},{1,17},{17,1},{2,18},{18,2},{3,19},{19,3},{4,20},{20... | collective-permute-start | bytes 5898248 | tf_op jit(solution)/shard_map/ppermute | solution.py:19
  102.7 3.5 copy-start.7
  105.7 10.8 %collective-permute-start.3 = (bf16[640,1536]{1,0:T(8,128)(2,1)}, bf16[640,1536]{1,0:T(8,128)(2,1)}, u32[]{:S(2)}, u32[]{:S(2)}) collective-permute-start(bf16[640,1536]{1,0:T(8,128)(2,1)} %pad_maximum_fusion.2), channel_id=1, source_target_pairs={{0,16},{16,0},{1,17},{17,1},{2,18},{18,2},{3,19},{19,3},{4,20},{20... | collective-permute-start | bytes 5898248 | tf_op jit(solution)/shard_map/ppermute | solution.py:19
  110.8 1.2 copy-start.9
  110.8 1.5 copy-start.13
  111.0 5.5 copy-start.10
  124.5 2.4 copy-start.22
  124.5 2.6 copy-start.18
  124.5 2.6 copy-start.19
  124.5 2.6 copy-start.20
  124.5 109.9 %copy-start.15 = (bf16[128,128,1]{0,1,2:T(8,128)(2,1)S(1)}, bf16[128,128,1]{0,1,2:T(8,128)(2,1)}, u32[]{:S(2)}) copy-start(bf16[128,128,1]{0,1,2:T(8,128)(2,1)} %constant.123) | copy-start | bytes 98308
  124.5 200.4 %all-gather.4.cloned.1.call-start = ((), (), s32[]{:S(2)}) async-start(), calls=%async_computation.6 | async-start | bytes 2457600 | tf_op jit(solution)/shard_map/all_gather | solution.py:102
  124.5 156.1 %collective-permute-start.7 = (bf16[320,1536]{1,0:T(8,128)(2,1)}, bf16[320,1536]{1,0:T(8,128)(2,1)}, u32[]{:S(2)}, u32[]{:S(2)}) collective-permute-start(bf16[320,1536]{1,0:T(8,128)(2,1)} %param.29), channel_id=1, source_target_pairs={{0,2},{2,0},{1,3},{3,1},{4,6},{6,4},{5,7},{7,5},{8,10},{10,8},{9,1... | collective-permute-start | bytes 2949128 | tf_op jit(solution)/shard_map/ppermute | solution.py:19
  238.8 23.9 %collective-permute-start.6 = (bf16[640,768]{1,0:T(8,128)(2,1)}, bf16[640,768]{1,0:T(8,128)(2,1)}, u32[]{:S(2)}, u32[]{:S(2)}) collective-permute-start(bf16[640,768]{1,0:T(8,128)(2,1)} %pad_maximum_fusion.8), channel_id=1, source_target_pairs={{0,2},{2,0},{1,3},{3,1},{4,6},{6,4},{5,7},{7,5},{8,10},{10,8},{9,1... | collective-permute-start | bytes 2949128 | tf_op jit(solution)/shard_map/ppermute | solution.py:19
  264.0 4.8 copy-start.4
  268.8 6.9 %copy-start.6 = (bf16[1280,384]{0,1:T(8,128)(2,1)S(1)}, bf16[1280,384]{0,1:T(8,128)(2,1)}, u32[]{:S(2)}) copy-start(bf16[1280,384]{0,1:T(8,128)(2,1)} %copy.104) | copy-start | bytes 2949124
  279.6 4.0 copy-start.11
  283.5 45.5 %collective-permute-start.8 = (bf16[640,1536]{1,0:T(8,128)(2,1)}, bf16[640,1536]{1,0:T(8,128)(2,1)}, u32[]{:S(2)}, u32[]{:S(2)}) collective-permute-start(bf16[640,1536]{1,0:T(8,128)(2,1)} %pad_maximum_fusion.5), channel_id=1, source_target_pairs={{0,16},{16,0},{1,17},{17,1},{2,18},{18,2},{3,19},{19,3},{4,20},{20... | collective-permute-start | bytes 5898248 | tf_op jit(solution)/shard_map/ppermute | solution.py:19
  283.5 52.5 %collective-permute-start.10 = (bf16[320,1536]{1,0:T(8,128)(2,1)S(1)}, bf16[320,1536]{1,0:T(8,128)(2,1)}, u32[]{:S(2)}, u32[]{:S(2)}) collective-permute-start(bf16[320,1536]{1,0:T(8,128)(2,1)S(1)} %copy-done.11), channel_id=1, source_target_pairs={{0,2},{2,0},{1,3},{3,1},{4,6},{6,4},{5,7},{7,5},{8,10},{10,8},{9,1... | collective-permute-start | bytes 2949128 | tf_op jit(solution)/shard_map/ppermute | solution.py:19
  334.5 37.6 %collective-permute-start.9 = (bf16[640,1280]{1,0:T(8,128)(2,1)S(1)}, bf16[640,1280]{1,0:T(8,128)(2,1)S(1)}, u32[]{:S(2)}, u32[]{:S(2)}) collective-permute-start(bf16[640,1280]{1,0:T(8,128)(2,1)S(1)} %fusion.47), channel_id=1, source_target_pairs={{0,1},{1,0},{2,3},{3,2},{4,5},{5,4},{6,7},{7,6},{8,9},{9,8},{10,11... | collective-permute-start | bytes 4915208 | tf_op jit(solution)/shard_map/ppermute | solution.py:19
  338.7 46.1 %collective-permute-start.11 = (bf16[640,1536]{1,0:T(8,128)(2,1)}, bf16[640,1536]{1,0:T(8,128)(2,1)}, u32[]{:S(2)}, u32[]{:S(2)}) collective-permute-start(bf16[640,1536]{1,0:T(8,128)(2,1)} %pad_maximum_fusion.6), channel_id=1, source_target_pairs={{0,16},{16,0},{1,17},{17,1},{2,18},{18,2},{3,19},{19,3},{4,20},{20... | collective-permute-start | bytes 5898248 | tf_op jit(solution)/shard_map/ppermute | solution.py:19
  391.9 46.6 %all-to-all-start.1 = ((bf16[4,640,384]{2,1,0:T(8,128)(2,1)}), bf16[4,640,384]{2,1,0:T(8,128)(2,1)S(1)}, u32[]{:S(2)}, u32[]{:S(2)}) async-start(bf16[4,640,384]{2,1,0:T(8,128)(2,1)} %bitcast.120), calls=%async_computation.2 | async-start | bytes 3932160 | tf_op jit(solution)/shard_map/all_to_all | solution.py:97
  395.5 98.2 %all-gather.6.cloned.1.call-start = ((), (), s32[]{:S(2)}) async-start(), calls=%async_computation.7 | async-start | bytes 2457600 | tf_op jit(solution)/shard_map/all_gather | solution.py:102
  395.6 55.7 %collective-permute-start.12 = (bf16[320,1536]{1,0:T(8,128)(2,1)}, bf16[320,1536]{1,0:T(8,128)(2,1)}, u32[]{:S(2)}, u32[]{:S(2)}) collective-permute-start(bf16[320,1536]{1,0:T(8,128)(2,1)} %param.31), channel_id=1, source_target_pairs={{0,2},{2,0},{1,3},{3,1},{4,6},{6,4},{5,7},{7,5},{8,10},{10,8},{9,1... | collective-permute-start | bytes 2949128 | tf_op jit(solution)/shard_map/ppermute | solution.py:19
  400.2 3.8 copy-start.21
  441.4 6.2 %copy-start.5 = (bf16[1,1,2048,384]{2,3,1,0:T(8,128)(2,1)S(1)}, bf16[1,1,2048,384]{2,3,1,0:T(8,128)(2,1)}, u32[]{:S(2)}) copy-start(bf16[1,1,2048,384]{2,3,1,0:T(8,128)(2,1)} %copy.134) | copy-start | bytes 4718596
  452.9 44.8 %collective-permute-start.13 = (bf16[640,1536]{1,0:T(8,128)(2,1)S(1)}, bf16[640,1536]{1,0:T(8,128)(2,1)}, u32[]{:S(2)}, u32[]{:S(2)}) collective-permute-start(bf16[640,1536]{1,0:T(8,128)(2,1)S(1)} %pad_maximum_fusion.7), channel_id=1, source_target_pairs={{0,16},{16,0},{1,17},{17,1},{2,18},{18,2},{3,19},{19,3},{4,20},{20... | collective-permute-start | bytes 5898248 | tf_op jit(solution)/shard_map/ppermute | solution.py:19
  504.4 37.9 %copy-start.1 = (f32[640,1280]{1,0:T(8,128)S(1)}, f32[640,1280]{1,0:T(8,128)}, u32[]{:S(2)}) copy-start(f32[640,1280]{1,0:T(8,128)} %get-tuple-element.17) | copy-start | bytes 9830404
  504.4 37.9 %collective-permute-start.14 = (bf16[640,1280]{1,0:T(8,128)(2,1)}, bf16[640,1280]{1,0:T(8,128)(2,1)}, u32[]{:S(2)}, u32[]{:S(2)}) collective-permute-start(bf16[640,1280]{1,0:T(8,128)(2,1)} %fusion.41), channel_id=1, source_target_pairs={{0,1},{1,0},{2,3},{3,2},{4,5},{5,4},{6,7},{7,6},{8,9},{9,8},{10,11... | collective-permute-start | bytes 4915208 | tf_op jit(solution)/shard_map/ppermute | solution.py:19
  547.9 19.0 %copy-start.14 = (bf16[1280,64,1]{0,1,2:T(8,128)(2,1)S(1)}, bf16[1280,64,1]{0,1,2:T(8,128)(2,1)}, u32[]{:S(2)}) copy-start(bf16[1280,64,1]{0,1,2:T(8,128)(2,1)} %reshape.480) | copy-start | bytes 491524
  569.7 14.3 %all-to-all-start.3 = ((f32[4,160,66]{1,2,0:T(8,128)}), f32[4,160,66]{1,2,0:T(8,128)S(1)}, u32[]{:S(2)}, u32[]{:S(2)}) async-start(f32[4,160,66]{1,2,0:T(8,128)} %pad_maximum_fusion.9), calls=%async_computation.4 | async-start | bytes 589824 | tf_op jit(solution)/shard_map/all_to_all | solution.py:97
  576.5 4.3 copy-start.2
  580.8 8.3 %copy-start.3 = (bf16[5120,64]{0,1:T(8,128)(2,1)S(1)}, bf16[5120,64]{0,1:T(8,128)(2,1)}, u32[]{:S(2)}) copy-start(bf16[5120,64]{0,1:T(8,128)(2,1)} %param.32) | copy-start | bytes 1966084
  580.8 10.0 %copy-start.16 = (f32[160,32]{0,1:T(8,128)S(1)}, f32[160,32]{0,1:T(8,128)}, u32[]{:S(2)}) copy-start(f32[160,32]{0,1:T(8,128)} %param.21) | copy-start | bytes 61444
  584.0 28.2 %all-to-all-start.2 = ((bf16[4,160,1,2,320]{4,3,2,1,0:T(2,128)(2,1)}), bf16[4,160,1,2,320]{4,3,2,1,0:T(2,128)(2,1)S(1)}, u32[]{:S(2)}, u32[]{:S(2)}) async-start(bf16[4,160,1,2,320]{4,3,2,1,0:T(2,128)(2,1)} %broadcast_select_fusion.3), calls=%async_computation.3 | async-start | bytes 1966080 | tf_op jit(solution)/shard_map/all_to_all | solution.py:97
  589.4 1.4 collective-permute-start.15
Sparse Core Ops, SparseCore 0:
  124.6 106.0 reduce-scatter.1
  280.7 44.0 all-gather.3
  451.3 42.3 all-gather.5

commit v2 on v1

v2 whole, which is shorter than its diff:
```python
import math

import jax
import jax.numpy as jnp
import numpy as np
from jax import lax
from jax.sharding import Mesh
from jax.sharding import PartitionSpec as P

HD = 128
TEXT = 512
TENANTS = 4
EPS = 1e-06
CHUNKS = 2
BF = jnp.bfloat16
F32 = jnp.float32


def flip(block, axis):
    return lax.ppermute(block, axis, [(0, 1), (1, 0)])


def rotary_tables():
    sixth = HD // 6
    table = np.zeros((3, HD), np.float32)
    lane = 0
    for column, span in enumerate((HD - 4 * sixth, 2 * sixth, 2 * sixth)):
        exponent = np.arange(0, span, 2).astype(np.float32) / np.float32(span)
        frequency = (1.0 / 10000.0**exponent).astype(np.float32)
        table[column, lane : lane + span] = np.repeat(frequency, 2)
        lane += span
    swap = np.zeros((HD, HD), np.float32)
    for pair in range(0, HD, 2):
        swap[pair + 1, pair] = -1.0
        swap[pair, pair + 1] = 1.0
    return table, swap


def head_scale(shaped):
    return lax.rsqrt(jnp.mean(shaped * shaped, axis=-1, keepdims=True) + EPS)


def attend(queries, keys, values, allowed):
    scores = jnp.einsum("qhd,khd->hqk", queries, keys, preferred_element_type=F32)
    scores = scores * (1.0 / math.sqrt(queries.shape[-1]))
    weights = jnp.where(allowed[None], jnp.exp(scores), 0.0).astype(BF)
    summed = jnp.einsum("hqk,khd->qhd", weights, values, preferred_element_type=F32)
    totals = jnp.sum(weights.astype(F32), axis=2).T
    return (summed / totals[..., None]).astype(BF).reshape(queries.shape[0], -1)


def on_device(
    hidden,
    latent,
    tenant_lengths,
    grid_positions,
    text_kv,
    text_lengths,
    w_query,
    w_key,
    w_value,
    w_out,
    w_cross_query,
    w_cross_out,
    w_head,
    guidance,
    step_size,
):
    halves, groups, parts, columns = (lax.axis_size(a) for a in ("cfg", "z", "t", "wt"))
    half_index, z_index, t_index, wt_index = (
        lax.axis_index(a) for a in ("cfg", "z", "t", "wt")
    )
    tok, width = hidden.shape[1:]
    rows = groups * tok
    local_cols = w_query.shape[1]
    my_cols = local_cols // groups
    heads = my_cols // HD
    paired = halves == 2 and parts == 2
    block = w_query.shape[0]
    ends = jnp.cumsum(tenant_lengths)

    def tenant_of(indices):
        return jnp.sum((indices[:, None] >= ends[None, :]).astype(jnp.int32), axis=1)

    def ordered(mine, other, index):
        return jnp.where(
            index == 0, jnp.concatenate([mine, other]), jnp.concatenate([other, mine])
        )

    def wide(w):
        if not paired:
            return lax.all_gather(w, ("cfg", "t"), axis=0, tiled=True)
        two = ordered(w, flip(w, "t"), t_index)
        return ordered(two, flip(two, "cfg"), half_index)

    def over_groups(x):
        return x if groups == 1 else lax.all_to_all(x, "z", 0, 0, tiled=True)

    def join_groups(x):
        if groups == 1:
            return x
        x = lax.all_gather(x, "z", axis=0)
        return jnp.swapaxes(x, 0, 1).reshape(x.shape[1], local_cols)

    def sum_at_owner(x):
        if groups == 1:
            return x[0].astype(F32)
        return jnp.sum(lax.all_to_all(x, "z", 0, 0).astype(F32), axis=0)

    def sum_groups(x):
        if groups == 1:
            return x
        return lax.psum_scatter(x, "z", scatter_dimension=0, tiled=True)

    def to_groups(x, n):
        return jnp.swapaxes(x.reshape(x.shape[0], groups, n), 0, 1)

    def both_columns(terms):
        terms = terms.astype(BF)
        if columns == 1:
            return terms.astype(F32)
        if columns == 2:
            return terms.astype(F32) + flip(terms, "wt").astype(F32)
        return lax.psum(terms, "wt").astype(F32)

    wide_query, wide_key, wide_value = wide(w_query), wide(w_key), wide(w_value)
    wide_out, wide_cross, wide_cross_out = wide(w_out), wide(w_cross_query), wide(w_cross_out)

    chunks = CHUNKS if groups > 1 and tok % (CHUNKS * 16) == 0 else 1
    part = tok // chunks
    chunk_rows = rows // chunks

    def by_chunk(x):
        shape = (groups, chunks, part) + x.shape[2:]
        return jnp.swapaxes(x.reshape(shape), 0, 1).reshape((rows,) + x.shape[2:])

    own = hidden[0].astype(F32)
    mean = jnp.mean(own, axis=-1, keepdims=True)
    centred = own - mean
    scale = lax.rsqrt(jnp.mean(centred * centred, axis=-1, keepdims=True) + EPS)
    facts = jnp.concatenate([mean, scale, grid_positions.astype(F32)], axis=1)
    slice_width = width // groups
    if groups == 1:
        sliced = own
    else:
        high = lax.reduce_precision(facts, 8, 7)
        middle = lax.reduce_precision(facts - high, 8, 7)
        low = facts - high - middle
        extra = jnp.concatenate([high, middle, low], axis=1).astype(BF)
        extra = jnp.pad(extra, ((0, 0), (0, 128 - extra.shape[1])))
        features = hidden[0].reshape(tok, halves, groups, slice_width // halves)
        features = jnp.concatenate(
            [features[:, half] for half in range(halves)]
            + [jnp.broadcast_to(extra[:, None], (tok, groups, 128))],
            axis=2,
        )
        arrived = lax.all_to_all(jnp.swapaxes(features, 0, 1), "z", 0, 0)
        arrived = by_chunk(arrived).astype(F32)
        sliced = arrived[:, :slice_width]
        extra = arrived[:, slice_width : slice_width + 15]
        facts = extra[:, 0:5] + extra[:, 5:10] + extra[:, 10:15]
    normed = ((sliced - facts[:, 0:1]) * facts[:, 1:2]).astype(BF)

    def project(w):
        return to_groups(jnp.dot(normed, w, preferred_element_type=F32).astype(BF), my_cols)

    projected_keys = sum_at_owner(project(wide_key)).astype(BF)
    projected = jnp.concatenate([project(wide_query), project(wide_value)], axis=2)
    projected = sum_groups(projected.reshape(groups * rows, 2 * my_cols))

    table, swap = rotary_tables()
    angles = (
        facts[:, 2:3] * table[0][None] + facts[:, 3:4] * table[1][None] + facts[:, 4:5] * table[2][None]
    )
    cosine, sinus = jnp.cos(angles)[:, None, :], jnp.sin(angles)[:, None, :]

    def rotated(x):
        shaped = x.reshape(rows, heads, HD)
        swapped = jnp.einsum("thd,de->the", shaped, jnp.asarray(swap, BF), preferred_element_type=F32)
        shaped = shaped.astype(F32)
        return ((shaped * cosine + swapped * sinus) * head_scale(shaped)).astype(BF)

    keys = rotated(projected_keys).reshape(rows, my_cols)
    queries = rotated(projected[:, :my_cols])
    values = projected[:, my_cols:]

    base = jnp.arange(groups, dtype=jnp.int32)[:, None] * (parts * tok)
    base = by_chunk(base + jnp.arange(tok, dtype=jnp.int32)[None])
    my_tenant = tenant_of(base + t_index * tok)
    if parts == 2:
        keys = jnp.concatenate([keys, flip(keys, "t")], axis=0)
        values = jnp.concatenate([values, flip(values, "t")], axis=0)
        key_tenant = jnp.concatenate([my_tenant, tenant_of(base + (1 - t_index) * tok)])
    else:
        keys = lax.all_gather(keys, "t", axis=0, tiled=True)
        values = lax.all_gather(values, "t", axis=0, tiled=True)
        key_tenant = tenant_of(
            (jnp.arange(parts, dtype=jnp.int32)[:, None] * tok + base[None]).reshape(-1)
        )
    keys = keys.reshape(-1, heads, HD)
    values = values.reshape(-1, heads, HD)

    spans = [slice(i * chunk_rows, (i + 1) * chunk_rows) for i in range(chunks)]
    mixed = [
        attend(queries[i], keys, values, my_tenant[i][:, None] == key_tenant[None, :])
        for i in spans
    ]

    def project_out(mixed, weight):
        return lax.dot_general(
            join_groups(mixed), weight, (((1,), (1,)), ((), ())), preferred_element_type=F32
        )

    column_sums = jnp.dot(jnp.ones((8, slice_width), BF), wide_cross, preferred_element_type=F32)
    column_sums = sum_at_owner(column_sums[0].reshape(groups, 1, my_cols))

    text = lax.dynamic_slice_in_dim(text_kv[:, 0], z_index * my_cols, my_cols, 2)
    text_keys = text[0].reshape(-1, heads, HD).astype(F32)
    text_keys = (text_keys * head_scale(text_keys)).astype(BF)
    text_values = text[1].reshape(-1, heads, HD)
    text_index = jnp.arange(text_kv.shape[2], dtype=jnp.int32)
    text_tenant = text_index // TEXT
    slots = text_tenant[:, None] == jnp.arange(TENANTS, dtype=jnp.int32)[None, :]
    live_length = jnp.sum(jnp.where(slots, text_lengths[0][None, :], 0), axis=1)
    live = text_index % TEXT < live_length

    states, cross_mixed = [], []
    for i, block_mixed in zip(spans, mixed):
        shifted = (sliced[i] - facts[i, 0:1]) + both_columns(project_out(block_mixed, wide_out))
        states.append(shifted)
        sums = jnp.stack([jnp.sum(shifted, axis=1), jnp.sum(shifted * shifted, axis=1)])
        sums = sum_at_owner(jnp.broadcast_to(sums[None], (groups,) + sums.shape)) / width
        crossed = jnp.dot(shifted.astype(BF), wide_cross, preferred_element_type=F32).astype(BF)
        crossed = sum_at_owner(to_groups(crossed, my_cols))
        variance = jnp.maximum(sums[1] - sums[0] * sums[0], 0.0)[:, None, None]
        shaped = (crossed - sums[0][:, None] * column_sums).reshape(chunk_rows, heads, HD)
        square = jnp.mean(shaped * shaped, axis=-1, keepdims=True)
        cross_queries = (shaped * lax.rsqrt(square + EPS * (variance + EPS))).astype(BF)
        allowed = (my_tenant[i][:, None] == text_tenant[None, :]) & live[None]
        cross_mixed.append(attend(cross_queries, text_keys, text_values, allowed))

    channels = w_head.shape[1]
    head_rows = lax.dynamic_index_in_dim(
        w_head.reshape(halves, groups, parts * block, channels), z_index, 1, keepdims=False
    ).reshape(-1, channels)
    totals = jnp.sum(w_head.astype(F32), axis=0)[None]
    out_width = width // columns

    leaving, velocity = [], []
    for i, shifted, block_mixed in zip(spans, states, cross_mixed):
        shifted = shifted + both_columns(project_out(block_mixed, wide_cross_out))
        final = (shifted + facts[i, 0:1]).astype(BF)
        if groups == 1:
            leaving.append(lax.dynamic_slice_in_dim(final, wt_index * out_width, out_width, 1))
        else:
            final = final.reshape(groups, part, slice_width)
            if columns == halves:
                span = slice_width // halves
                final = lax.dynamic_slice_in_dim(final, wt_index * span, span, 2)
            final = jnp.swapaxes(lax.all_to_all(final, "z", 0, 0), 0, 1)
            if columns == halves:
                leaving.append(final.reshape(part, out_width))
            else:
                final = final.reshape(part, groups, halves, -1)
                final = jnp.swapaxes(final, 1, 2).reshape(part, width)
                leaving.append(
                    lax.dynamic_slice_in_dim(final, wt_index * out_width, out_width, 1)
                )
        sums = jnp.concatenate(
            [
                jnp.dot(shifted.astype(BF), head_rows, preferred_element_type=F32),
                jnp.sum(shifted, axis=1, keepdims=True),
                jnp.sum(shifted * shifted, axis=1, keepdims=True),
            ],
            axis=1,
        )
        sums = sum_at_owner(sums.reshape(groups, part, channels + 2))
        mean = sums[:, channels : channels + 1] / width
        variance = jnp.maximum(sums[:, channels + 1 :] / width - mean * mean, 0.0)
        velocity.append((sums[:, :channels] - mean * totals) * lax.rsqrt(variance + EPS))
    hidden_out = jnp.concatenate(leaving)
    velocity = jnp.concatenate(velocity)

    channel_half = latent.shape[1]
    outgoing = lax.dynamic_slice_in_dim(velocity, (1 - half_index) * channel_half, channel_half, 1)
    partner = flip(outgoing, "cfg")
    own_part = lax.dynamic_slice_in_dim(velocity, half_index * channel_half, channel_half, 1)
    conditional = jnp.where(half_index == 0, own_part, partner)
    null_text = jnp.where(half_index == 0, partner, own_part)
    latent_next = latent + step_size[0] * (null_text + guidance[0] * (conditional - null_text))
    return (hidden_out[None], latent_next)


def solution(mesh):
    halves, seq, columns = (mesh.shape[a] for a in ("cfg", "seq", "wt"))

    def run(*args):
        heads_here = args[6].shape[1] // columns // HD
        groups = math.gcd(heads_here, seq)
        fine = Mesh(
            mesh.devices.reshape(halves, groups, seq // groups, columns), ("cfg", "z", "t", "wt")
        )
        seq_axes = ("z", "t")
        weight = P(("cfg", "z", "t"), "wt")
        return jax.shard_map(
            on_device,
            mesh=fine,
            in_specs=(
                P("cfg", seq_axes, None),
                P(seq_axes, "cfg"),
                P(),
                P(seq_axes, None),
                P(None, "cfg", None, "wt"),
                P("cfg", None),
                weight,
                weight,
                weight,
                weight,
                weight,
                weight,
                P(),
                P(),
                P(),
            ),
            out_specs=(P("cfg", seq_axes, "wt"), P(seq_axes, "cfg")),
            check_vma=False,
        )(*args)

    return run
```

time: 629 us -> 514 us (0.82)
  waiting for transfers between devices: 333 us -> 181 us
  local copies, waits for them, and re-layouts: 97.8 us -> 46.7 us
  blocking collectives: 34.1 us -> 75 us
  starting transfers between devices: 31.7 us -> 62.1 us
  matrix products: 54.6 us -> 72.1 us
    reduce_scatter x1, waiting for transfers between devices: 102 us -> 0.02 us  [sum_groups(): return lax.psum_scatter(x, 'z', scatter_dimension=0, tiled=True)]
    all_gather x2 -> x0, waiting for transfers between devices: 80.6 us -> none  [join_groups(): x = lax.all_gather(x, 'z', axis=0)]
    all_to_all x4 -> x11, waiting for transfers between devices: 52.2 us -> 128 us  [the longest x8 111 us: sum_at_owner(): return jnp.sum(lax.all_to_all(x, 'z', 0, 0).astype(F32), axis=0)]
    all_gather x1 -> x4, blocking collectives: 24 us -> 75 us  [join_groups(): x = lax.all_gather(x, 'z', axis=0)]
    ppermute x16 -> x19, waiting for transfers between devices: 98.7 us -> 53.3 us  [flip(): return lax.ppermute(block, axis, [(0, 1), (1, 0)])]
    rev x4 -> x0, local copies, waits for them, and re-layouts: 38.6 us -> none  [the longest x1 18.2 us: local_order(): x = jnp.where(t_index == 1, x[..., ::-1, :], x)]
    all_to_all x4 -> x11, starting transfers between devices: 17 us -> 45.9 us  [the longest x8 32.7 us: sum_at_owner(): return jnp.sum(lax.all_to_all(x, 'z', 0, 0).astype(F32), axis=0)]
    concatenate x10 -> x4, other arithmetic: 20.1 us -> 2.38 us  [the longest x1 2.19 us: on_device(): jnp.concatenate([project(wide_query), project(wide_value)], axis=2)]
  transfers between devices with their start and end apart: 23 -> 31, of which waited for: 9 -> 15; matrix products, arithmetic and copies ran while one was open for 24% -> 30% of each run, Pallas kernels for 0% -> 0%
where the time goes in v2:
time: 514 us; the launch traced here: 509 us
  waiting for transfers between devices  181 us (35%)
  blocking collectives  75 us (15%)
  matrix products  72.1 us (14%)
  starting transfers between devices  62.1 us (12%)
  other arithmetic  55.2 us (11%)
  local copies, waits for them, and re-layouts  46.7 us (9%)
  between operations  16.5 us (3%)
    all_to_all x8, waiting for transfers between devices, sum_at_owner(): return jnp.sum(lax.all_to_all(x, 'z', 0, 0).astype(F32), axis=0)  111 us
    all_gather x4, blocking collectives, join_groups(): x = lax.all_gather(x, 'z', axis=0)  75 us
    ppermute x19, waiting for transfers between devices, flip(): return lax.ppermute(block, axis, [(0, 1), (1, 0)])  53.3 us
    all_to_all x8, starting transfers between devices, sum_at_owner(): return jnp.sum(lax.all_to_all(x, 'z', 0, 0).astype(F32), axis=0)  32.7 us
    select_n x6, other arithmetic, ordered(): jnp.where(index == 0, jnp.concatenate([mine, other]), jnp.concatenate([ot...  20.5 us
    dot_general x4, matrix products, project_out(): lax.dot_general(join_groups(mixed), weight, (((1,), (1,)), ((), ())), pre...  19.6 us
    all_to_all x2, waiting for transfers between devices, on_device(): final = jnp.swapaxes(lax.all_to_all(final, 'z', 0, 0), 0, 1)  16.9 us
    ppermute x19, starting transfers between devices, flip(): return lax.ppermute(block, axis, [(0, 1), (1, 0)])  15.7 us
  transfers between devices with their start and end apart: 31, of which 15 were waited for; matrix products, arithmetic and copies ran while one was open for 30% of the time, Pallas kernels for 0%

profile of v2, /device:TPU:0, one launch (start us, length us, event | category | flops | bytes accessed | tf_op | source)
XLA Modules:
  0.0 508.9 jit_solution(4540591037341607597)
XLA Ops:
  9.0 3.3 reshape_squeeze.10
  16.2 6.3 %all-to-all-start = ((bf16[4,160,1408]{2,1,0:T(8,128)(2,1)}), bf16[4,160,1408]{2,1,0:T(8,128)(2,1)S(1)}, u32[]{:S(2)}, u32[]{:S(2)}) async-start(bf16[4,160,1408]{2,1,0:T(8,128)(2,1)} %copy.202), calls=%async_computation | async-start | bytes 3604480 | tf_op jit(solution)/shard_map/all_to_all | solution.py:157
  26.6 21.3 %collective-permute-done = bf16[320,1536]{1,0:T(8,128)(2,1)} collective-permute-done((bf16[320,1536]{1,0:T(8,128)(2,1)S(1)}, bf16[320,1536]{1,0:T(8,128)(2,1)}, u32[]{:S(2)}, u32[]{:S(2)}) %collective-permute-start) | collective-permute-done | bytes 983072 | tf_op jit(solution)/shard_map/ppermute | solution.py:20
  47.9 3.4 maximum_select_fusion.15
  51.2 17.7 %collective-permute-done.2 = bf16[320,1536]{1,0:T(8,128)(2,1)} collective-permute-done((bf16[320,1536]{1,0:T(8,128)(2,1)}, bf16[320,1536]{1,0:T(8,128)(2,1)}, u32[]{:S(2)}, u32[]{:S(2)}) %collective-permute-start.2) | collective-permute-done | bytes 983072 | tf_op jit(solution)/shard_map/ppermute | solution.py:20
  68.9 3.4 maximum_select_fusion.16
  74.6 6.0 %fusion.28 = bf16[640,1536]{1,0:T(8,128)(2,1)S(1)} fusion(bf16[640,1280]{1,0:T(8,128)(2,1)S(1)} %fusion.25, bf16[640,1536]{1,0:T(8,128)(2,1)} %collective-permute-done.1, bf16[640,1536]{1,0:T(8,128)(2,1)} %maximum_select_fusion.15, pred[]{:T(512)S(6)} %eq.50), kind=kOutput, calls=%fused_computation.49 | convolution fusion | flops 2535260160 | bytes 7536641 | tf_op jit(solution)/shard_map/dot_general | solution.py:165
  80.7 6.1 %fusion.27 = bf16[640,1536]{1,0:T(8,128)(2,1)S(1)} fusion(bf16[640,1280]{1,0:T(8,128)(2,1)S(1)} %fusion.25, bf16[640,1536]{1,0:T(8,128)(2,1)} %collective-permute-done.3, bf16[640,1536]{1,0:T(8,128)(2,1)} %maximum_select_fusion.16, pred[]{:T(512)S(6)} %eq.50), kind=kOutput, calls=%fused_computation.48 | convolution fusion | flops 2535260160 | bytes 7536641 | tf_op jit(solution)/shard_map/dot_general | solution.py:165
  93.2 3.6 collective-permute-done.6
  96.8 3.0 fusion.26
  101.5 5.3 %all-to-all-start.1 = ((bf16[4,640,384]{2,1,0:T(8,128)(2,1)}), bf16[4,640,384]{2,1,0:T(8,128)(2,1)S(1)}, u32[]{:S(2)}, u32[]{:S(2)}) async-start(bf16[4,640,384]{2,1,0:T(8,128)(2,1)} %bitcast.175), calls=%async_computation.2 | async-start | bytes 3932160 | tf_op jit(solution)/shard_map/all_to_all | solution.py:108
  110.8 3.9 constant_dynamic-slice_fusion.3
  124.6 76.0 %all-to-all-done.1 = bf16[4,640,384]{2,1,0:T(8,128)(2,1)S(1)} async-done(((bf16[4,640,384]{2,1,0:T(8,128)(2,1)}), bf16[4,640,384]{2,1,0:T(8,128)(2,1)S(1)}, u32[]{:S(2)}, u32[]{:S(2)}) %all-to-all-start.1) | async-done | bytes 1966112 | tf_op jit(solution)/shard_map/all_to_all | solution.py:108
  204.4 3.9 maximum_select_fusion.18
  208.3 4.0 maximum_select_fusion.19
  219.8 4.0 convert_reduce_fusion.2
  233.2 19.8 %all_gather.14 = bf16[4,320,384]{2,1,0:T(8,128)(2,1)S(1)} all-gather(bf16[1,320,384]{2,1,0:T(8,128)(2,1)S(1)} %copy.238), channel_id=1, replica_groups=mesh['cfg'=2,'z'=4,'t'=2,'wt'=2] {'z'}, dimensions={0}, use_global_device_ids=true | all-gather | bytes 1228800 | tf_op jit(solution)/shard_map/all_gather | solution.py:102
  253.1 4.4 convolution_convert_fusion.2
  260.4 18.3 %all_gather.12 = bf16[4,320,384]{2,1,0:T(8,128)(2,1)S(1)} all-gather(bf16[1,320,384]{2,1,0:T(8,128)(2,1)S(1)} %copy.221), channel_id=1, replica_groups=mesh['cfg'=2,'z'=4,'t'=2,'wt'=2] {'z'}, dimensions={0}, use_global_device_ids=true | all-gather | bytes 1228800 | tf_op jit(solution)/shard_map/all_gather | solution.py:102
  278.8 4.4 convolution_convert_fusion.5
  284.2 5.1 %fusion.76 = f32[1,1536]{1,0:T(1,128)} fusion(bf16[640,1536]{1,0:T(8,128)(2,1)} %collective-permute-done.12, bf16[640,1536]{1,0:T(8,128)(2,1)} %maximum_select_fusion.19, pred[]{:T(512)S(6)} %eq.50), kind=kOutput, calls=%fused_computation.195 | convolution fusion | flops 21626880 | bytes 3938305 | tf_op jit(solution)/shard_map/dot_general | solution.py:214
  289.3 4.1 all-to-all-start.4
  293.4 3.2 collective-permute-done.10
  297.5 3.8 fusion.94
  302.0 3.7 all-to-all-start.3
  305.7 5.6 %all-to-all-done.3 = f32[4,2,320]{2,1,0:T(2,128)S(1)} async-done(((f32[4,2,320]{2,1,0:T(2,128)}), f32[4,2,320]{2,1,0:T(2,128)S(1)}, u32[]{:S(2)}, u32[]{:S(2)}) %all-to-all-start.3) | async-done | bytes 10272 | tf_op jit(solution)/shard_map/all_to_all | solution.py:108
  311.9 3.3 all-to-all-start.7
  315.1 5.0 convolution_convert_fusion.4
  321.2 5.1 all-to-all-start.2
  328.3 5.0 convolution_convert_fusion.1
  334.4 14.1 %all-to-all-done.2 = bf16[4,320,384]{2,1,0:T(8,128)(2,1)} async-done(((bf16[4,320,384]{2,1,0:T(8,128)(2,1)}), bf16[4,320,384]{2,1,0:T(8,128)(2,1)}, u32[]{:S(2)}, u32[]{:S(2)}) %all-to-all-start.2) | async-done | bytes 983072 | tf_op jit(solution)/shard_map/all_to_all | solution.py:108
  348.4 4.6 all-to-all-start.6
  353.1 3.9 maximum_select_fusion.20
  362.0 6.3 %all-to-all-done.6 = bf16[4,320,384]{2,1,0:T(8,128)(2,1)} async-done(((bf16[4,320,384]{2,1,0:T(8,128)(2,1)}), bf16[4,320,384]{2,1,0:T(8,128)(2,1)}, u32[]{:S(2)}, u32[]{:S(2)}) %all-to-all-start.6) | async-done | bytes 983072 | tf_op jit(solution)/shard_map/all_to_all | solution.py:108
  374.7 4.6 convert_reduce_fusion.1
  382.6 18.6 %all_gather.13 = bf16[4,320,384]{2,1,0:T(8,128)(2,1)S(1)} all-gather(bf16[1,320,384]{2,1,0:T(8,128)(2,1)S(1)} %copy.233), channel_id=1, replica_groups=mesh['cfg'=2,'z'=4,'t'=2,'wt'=2] {'z'}, dimensions={0}, use_global_device_ids=true | all-gather | bytes 1228800 | tf_op jit(solution)/shard_map/all_gather | solution.py:102
  401.4 5.3 %convolution_convert_fusion.3 = bf16[320,1280]{1,0:T(8,128)(2,1)} fusion(bf16[320,1536]{1,0:T(8,128)(2,1)S(1)} %bitcast.216, bf16[640,1536]{1,0:T(8,128)(2,1)} %collective-permute-done.14, bf16[640,1536]{1,0:T(8,128)(2,1)} %maximum_select_fusion.20, pred[]{:T(512)S(6)} %eq.50), kind=kOutput, calls=%fused_computation.55 | convolution fusion | flops 1276395520 | bytes 5734401 | tf_op jit(solution)/shard_map/dot_general | solution.py:210
  407.7 3.1 convert_reduce_fusion
  414.0 18.3 %all_gather.15 = bf16[4,320,384]{2,1,0:T(8,128)(2,1)S(1)} all-gather(bf16[1,320,384]{2,1,0:T(8,128)(2,1)S(1)} %copy.248), channel_id=1, replica_groups=mesh['cfg'=2,'z'=4,'t'=2,'wt'=2] {'z'}, dimensions={0}, use_global_device_ids=true | all-gather | bytes 1228800 | tf_op jit(solution)/shard_map/all_gather | solution.py:102
  432.4 5.5 %convolution_convert_fusion = bf16[320,1280]{1,0:T(8,128)(2,1)} fusion(bf16[320,1536]{1,0:T(8,128)(2,1)S(1)} %bitcast.218, bf16[640,1536]{1,0:T(8,128)(2,1)} %collective-permute-done.14, bf16[640,1536]{1,0:T(8,128)(2,1)} %maximum_select_fusion.20, pred[]{:T(512)S(6)} %eq.50), kind=kOutput, calls=%fused_computation.52 | convolution fusion | flops 1276395520 | bytes 5734401 | tf_op jit(solution)/shard_map/dot_general | solution.py:210
  454.9 3.3 all-to-all-start.9
  459.6 4.6 all-to-all-done.9
  464.2 3.3 all-to-all-start.10
  469.4 4.4 all-to-all-done.10
  473.7 3.5 all-to-all-start.5
  478.3 10.2 %all-to-all-done.5 = bf16[4,80,640]{2,1,0:T(8,128)(2,1)S(1)} async-done(((bf16[4,80,640]{2,1,0:T(8,128)(2,1)}), bf16[4,80,640]{2,1,0:T(8,128)(2,1)S(1)}, u32[]{:S(2)}, u32[]{:S(2)}) %all-to-all-start.5) | async-done | bytes 409632 | tf_op jit(solution)/shard_map/all_to_all | solution.py:260
  488.4 3.5 all-to-all-start.8
  494.2 6.7 %all-to-all-done.8 = bf16[4,80,640]{2,1,0:T(8,128)(2,1)S(1)} async-done(((bf16[4,80,640]{2,1,0:T(8,128)(2,1)}), bf16[4,80,640]{2,1,0:T(8,128)(2,1)S(1)}, u32[]{:S(2)}, u32[]{:S(2)}) %all-to-all-start.8) | async-done | bytes 409632 | tf_op jit(solution)/shard_map/all_to_all | solution.py:260
  (239 shorter events, 106.6 us)
Async XLA Ops:
  14.7 8.3 %copy-start.8 = (bf16[320,1536]{1,0:T(8,128)(2,1)S(1)}, bf16[320,1536]{1,0:T(8,128)(2,1)}, u32[]{:S(2)}) copy-start(bf16[320,1536]{1,0:T(8,128)(2,1)} %param.26) | copy-start | bytes 2949124
  16.2 56.1 %all-to-all-start = ((bf16[4,160,1408]{2,1,0:T(8,128)(2,1)}), bf16[4,160,1408]{2,1,0:T(8,128)(2,1)S(1)}, u32[]{:S(2)}, u32[]{:S(2)}) async-start(bf16[4,160,1408]{2,1,0:T(8,128)(2,1)} %copy.202), calls=%async_computation | async-start | bytes 3604480 | tf_op jit(solution)/shard_map/all_to_all | solution.py:157
  22.5 193.1 %reduce-scatter.2.cloned.1.call-start = ((), (), s32[]{:S(2)}) async-start(), calls=%async_computation.12 | async-start | bytes 4915200 | tf_op jit(solution)/shard_map/reduce_scatter | solution.py:113
  23.0 24.9 %collective-permute-start = (bf16[320,1536]{1,0:T(8,128)(2,1)S(1)}, bf16[320,1536]{1,0:T(8,128)(2,1)}, u32[]{:S(2)}, u32[]{:S(2)}) collective-permute-start(bf16[320,1536]{1,0:T(8,128)(2,1)S(1)} %copy-done.8), channel_id=1, source_target_pairs={{0,2},{2,0},{1,3},{3,1},{4,6},{6,4},{5,7},{7,5},{8,10},{10,8},{9,1... | collective-permute-start | bytes 2949128 | tf_op jit(solution)/shard_map/ppermute | solution.py:20
  24.6 44.4 %collective-permute-start.2 = (bf16[320,1536]{1,0:T(8,128)(2,1)}, bf16[320,1536]{1,0:T(8,128)(2,1)}, u32[]{:S(2)}, u32[]{:S(2)}) collective-permute-start(bf16[320,1536]{1,0:T(8,128)(2,1)} %param.28), channel_id=1, source_target_pairs={{0,2},{2,0},{1,3},{3,1},{4,6},{6,4},{5,7},{7,5},{8,10},{10,8},{9,1... | collective-permute-start | bytes 2949128 | tf_op jit(solution)/shard_map/ppermute | solution.py:20
  25.1 64.3 %collective-permute-start.5 = (bf16[320,1536]{1,0:T(8,128)(2,1)}, bf16[320,1536]{1,0:T(8,128)(2,1)}, u32[]{:S(2)}, u32[]{:S(2)}) collective-permute-start(bf16[320,1536]{1,0:T(8,128)(2,1)} %param.27), channel_id=1, source_target_pairs={{0,2},{2,0},{1,3},{3,1},{4,6},{6,4},{5,7},{7,5},{8,10},{10,8},{9,1... | collective-permute-start | bytes 2949128 | tf_op jit(solution)/shard_map/ppermute | solution.py:20
  26.6 42.3 %copy-start.9 = (bf16[320,1536]{1,0:T(8,128)(2,1)S(1)}, bf16[320,1536]{1,0:T(8,128)(2,1)}, u32[]{:S(2)}) copy-start(bf16[320,1536]{1,0:T(8,128)(2,1)} %param.28) | copy-start | bytes 2949124
  51.2 23.4 %collective-permute-start.1 = (bf16[640,1536]{1,0:T(8,128)(2,1)}, bf16[640,1536]{1,0:T(8,128)(2,1)}, u32[]{:S(2)}, u32[]{:S(2)}) collective-permute-start(bf16[640,1536]{1,0:T(8,128)(2,1)} %maximum_select_fusion.15), channel_id=1, source_target_pairs={{0,16},{16,0},{1,17},{17,1},{2,18},{18,2},{3,19},{19,3},{4,20},{20... | collective-permute-start | bytes 5898248 | tf_op jit(solution)/shard_map/ppermute | solution.py:20
  72.3 8.4 %collective-permute-start.3 = (bf16[640,1536]{1,0:T(8,128)(2,1)}, bf16[640,1536]{1,0:T(8,128)(2,1)}, u32[]{:S(2)}, u32[]{:S(2)}) collective-permute-start(bf16[640,1536]{1,0:T(8,128)(2,1)} %maximum_select_fusion.16), channel_id=1, source_target_pairs={{0,16},{16,0},{1,17},{17,1},{2,18},{18,2},{3,19},{19,3},{4,20},{20... | collective-permute-start | bytes 5898248 | tf_op jit(solution)/shard_map/ppermute | solution.py:20
  92.7 4.2 collective-permute-start.6
  99.9 10.7 %copy-start.33 = (s32[4]{0:T(128)S(1)}, s32[4]{0:T(128)}, u32[]{:S(2)}) copy-start(s32[4]{0:T(128)} %param.22) | copy-start | bytes 52
  101.5 99.1 %all-to-all-start.1 = ((bf16[4,640,384]{2,1,0:T(8,128)(2,1)}), bf16[4,640,384]{2,1,0:T(8,128)(2,1)S(1)}, u32[]{:S(2)}, u32[]{:S(2)}) async-start(bf16[4,640,384]{2,1,0:T(8,128)(2,1)} %bitcast.175), calls=%async_computation.2 | async-start | bytes 3932160 | tf_op jit(solution)/shard_map/all_to_all | solution.py:108
  106.8 97.7 %collective-permute-start.8 = (bf16[320,1536]{1,0:T(8,128)(2,1)}, bf16[320,1536]{1,0:T(8,128)(2,1)}, u32[]{:S(2)}, u32[]{:S(2)}) collective-permute-start(bf16[320,1536]{1,0:T(8,128)(2,1)} %param.29), channel_id=1, source_target_pairs={{0,2},{2,0},{1,3},{3,1},{4,6},{6,4},{5,7},{7,5},{8,10},{10,8},{9,1... | collective-permute-start | bytes 2949128 | tf_op jit(solution)/shard_map/ppermute | solution.py:20
  108.3 99.9 %collective-permute-start.11 = (bf16[320,1536]{1,0:T(8,128)(2,1)}, bf16[320,1536]{1,0:T(8,128)(2,1)}, u32[]{:S(2)}, u32[]{:S(2)}) collective-permute-start(bf16[320,1536]{1,0:T(8,128)(2,1)} %param.30), channel_id=1, source_target_pairs={{0,2},{2,0},{1,3},{3,1},{4,6},{6,4},{5,7},{7,5},{8,10},{10,8},{9,1... | collective-permute-start | bytes 2949128 | tf_op jit(solution)/shard_map/ppermute | solution.py:20
  108.8 244.2 %collective-permute-start.13 = (bf16[320,1536]{1,0:T(8,128)(2,1)}, bf16[320,1536]{1,0:T(8,128)(2,1)}, u32[]{:S(2)}, u32[]{:S(2)}) collective-permute-start(bf16[320,1536]{1,0:T(8,128)(2,1)} %param.31), channel_id=1, source_target_pairs={{0,2},{2,0},{1,3},{3,1},{4,6},{6,4},{5,7},{7,5},{8,10},{10,8},{9,1... | collective-permute-start | bytes 2949128 | tf_op jit(solution)/shard_map/ppermute | solution.py:20
  121.9 80.2 %copy-start.16 = (bf16[128,128,1]{1,0,2:T(8,128)(2,1)S(1)}, bf16[128,128,1]{1,0,2:T(8,128)(2,1)}, u32[]{:S(2)}) copy-start(bf16[128,128,1]{1,0,2:T(8,128)(2,1)} %constant.136) | copy-start | bytes 98308
  202.8 12.4 %collective-permute-start.7 = (bf16[640,384]{0,1:T(8,128)(2,1)S(1)}, bf16[640,384]{0,1:T(8,128)(2,1)S(1)}, u32[]{:S(2)}, u32[]{:S(2)}) collective-permute-start(bf16[640,384]{0,1:T(8,128)(2,1)S(1)} %bitcast.222), channel_id=1, source_target_pairs={{0,2},{2,0},{1,3},{3,1},{4,6},{6,4},{5,7},{7,5},{8,10},{10,8},{9,1... | collective-permute-start | bytes 1474568 | tf_op jit(solution)/shard_map/ppermute | solution.py:20
  208.3 44.8 %collective-permute-start.9 = (bf16[640,1536]{1,0:T(8,128)(2,1)}, bf16[640,1536]{1,0:T(8,128)(2,1)}, u32[]{:S(2)}, u32[]{:S(2)}) collective-permute-start(bf16[640,1536]{1,0:T(8,128)(2,1)} %maximum_select_fusion.18), channel_id=1, source_target_pairs={{0,16},{16,0},{1,17},{17,1},{2,18},{18,2},{3,19},{19,3},{4,20},{20... | collective-permute-start | bytes 5898248 | tf_op jit(solution)/shard_map/ppermute | solution.py:20
  212.2 71.9 %collective-permute-start.12 = (bf16[640,1536]{1,0:T(8,128)(2,1)}, bf16[640,1536]{1,0:T(8,128)(2,1)}, u32[]{:S(2)}, u32[]{:S(2)}) collective-permute-start(bf16[640,1536]{1,0:T(8,128)(2,1)} %maximum_select_fusion.19), channel_id=1, source_target_pairs={{0,16},{16,0},{1,17},{17,1},{2,18},{18,2},{3,19},{19,3},{4,20},{20... | collective-permute-start | bytes 5898248 | tf_op jit(solution)/shard_map/ppermute | solution.py:20
  217.8 11.5 %collective-permute-start.4 = (bf16[640,384]{1,0:T(8,128)(2,1)S(1)}, bf16[640,384]{1,0:T(8,128)(2,1)S(1)}, u32[]{:S(2)}, u32[]{:S(2)}) collective-permute-start(bf16[640,384]{1,0:T(8,128)(2,1)S(1)} %get-tuple-element.41), channel_id=1, source_target_pairs={{0,2},{2,0},{1,3},{3,1},{4,6},{6,4},{5,7},{7,5},{8,10},{10,8},{9,1... | collective-permute-start | bytes 1474568 | tf_op jit(solution)/shard_map/ppermute | solution.py:20
  257.5 35.8 %collective-permute-start.16 = (bf16[320,1280]{1,0:T(8,128)(2,1)S(1)}, bf16[320,1280]{1,0:T(8,128)(2,1)}, u32[]{:S(2)}, u32[]{:S(2)}) collective-permute-start(bf16[320,1280]{1,0:T(8,128)(2,1)S(1)} %convolution_convert_fusion.2), channel_id=1, source_target_pairs={{0,1},{1,0},{2,3},{3,2},{4,5},{5,4},{6,7},{7,6},{8,9},{9,8},{10,11... | collective-permute-start | bytes 2457608 | tf_op jit(solution)/shard_map/ppermute | solution.py:20
  283.2 13.3 %collective-permute-start.10 = (bf16[320,1280]{1,0:T(8,128)(2,1)S(1)}, bf16[320,1280]{1,0:T(8,128)(2,1)S(1)}, u32[]{:S(2)}, u32[]{:S(2)}) collective-permute-start(bf16[320,1280]{1,0:T(8,128)(2,1)S(1)} %convolution_convert_fusion.5), channel_id=1, source_target_pairs={{0,1},{1,0},{2,3},{3,2},{4,5},{5,4},{6,7},{7,6},{8,9},{9,8},{10,11... | collective-permute-start | bytes 2457608 | tf_op jit(solution)/shard_map/ppermute | solution.py:20
  284.1 13.3 %copy-start.21 = (f32[320]{0:T(512)}, f32[320]{0:T(512)S(1)}, u32[]{:S(2)}) copy-start(f32[320]{0:T(512)S(1)} %get-tuple-element.10) | copy-start | bytes 3844
  284.2 13.3 %copy-start.23 = (f32[320]{0:T(512)}, f32[320]{0:T(512)S(1)}, u32[]{:S(2)}) copy-start(f32[320]{0:T(512)S(1)} %get-tuple-element.11) | copy-start | bytes 3844
  289.3 12.0 %all-to-all-start.4 = ((f32[4,1,384]{2,1,0:T(1,128)}), f32[4,1,384]{2,1,0:T(1,128)S(1)}, u32[]{:S(2)}, u32[]{:S(2)}) async-start(f32[4,1,384]{2,1,0:T(1,128)} %bitcast.30), calls=%async_computation.5 | async-start | bytes 12288 | tf_op jit(solution)/shard_map/all_to_all | solution.py:108
  302.0 9.3 %all-to-all-start.3 = ((f32[4,2,320]{2,1,0:T(2,128)}), f32[4,2,320]{2,1,0:T(2,128)S(1)}, u32[]{:S(2)}, u32[]{:S(2)}) async-start(f32[4,2,320]{2,1,0:T(2,128)} %broadcast_in_dim.67), calls=%async_computation.4 | async-start | bytes 24576 | tf_op jit(solution)/shard_map/all_to_all | solution.py:108
  311.9 9.3 %all-to-all-start.7 = ((f32[4,2,320]{2,1,0:T(2,128)}), f32[4,2,320]{2,1,0:T(2,128)S(1)}, u32[]{:S(2)}, u32[]{:S(2)}) async-start(f32[4,2,320]{2,1,0:T(2,128)} %broadcast_in_dim.72), calls=%async_computation.8 | async-start | bytes 24576 | tf_op jit(solution)/shard_map/all_to_all | solution.py:108
  321.2 27.2 %all-to-all-start.2 = ((bf16[4,320,384]{2,1,0:T(8,128)(2,1)}), bf16[4,320,384]{2,1,0:T(8,128)(2,1)}, u32[]{:S(2)}, u32[]{:S(2)}) async-start(bf16[4,320,384]{2,1,0:T(8,128)(2,1)} %bitcast.187), calls=%async_computation.3 | async-start | bytes 1966080 | tf_op jit(solution)/shard_map/all_to_all | solution.py:108
  348.4 19.9 %all-to-all-start.6 = ((bf16[4,320,384]{2,1,0:T(8,128)(2,1)}), bf16[4,320,384]{2,1,0:T(8,128)(2,1)}, u32[]{:S(2)}, u32[]{:S(2)}) async-start(bf16[4,320,384]{2,1,0:T(8,128)(2,1)} %bitcast.186), calls=%async_computation.7 | async-start | bytes 1966080 | tf_op jit(solution)/shard_map/all_to_all | solution.py:108
  357.0 44.3 %collective-permute-start.14 = (bf16[640,1536]{1,0:T(8,128)(2,1)}, bf16[640,1536]{1,0:T(8,128)(2,1)}, u32[]{:S(2)}, u32[]{:S(2)}) collective-permute-start(bf16[640,1536]{1,0:T(8,128)(2,1)} %maximum_select_fusion.20), channel_id=1, source_target_pairs={{0,16},{16,0},{1,17},{17,1},{2,18},{18,2},{3,19},{19,3},{4,20},{20... | collective-permute-start | bytes 5898248 | tf_op jit(solution)/shard_map/ppermute | solution.py:20
  357.1 17.7 %copy-start.25 = (f32[384]{0:T(512)}, f32[384]{0:T(512)S(1)}, u32[]{:S(2)}) copy-start(f32[384]{0:T(512)S(1)} %reduce_sum.300) | copy-start | bytes 4612
  357.2 17.5 %copy-start.19 = (f32[320]{0:T(512)}, f32[320]{0:T(512)S(1)}, u32[]{:S(2)}) copy-start(f32[320]{0:T(512)S(1)} %get-tuple-element.20) | copy-start | bytes 3844
  401.3 6.3 %copy-start.18 = (f32[320,3]{0,1:T(4,128)S(1)}, f32[320,3]{0,1:T(4,128)}, u32[]{:S(2)}) copy-start(f32[320,3]{0,1:T(4,128)} %get-tuple-element.22) | copy-start | bytes 11524
  401.3 6.3 %copy-start.27 = (f32[320]{0:T(512)S(1)}, f32[320]{0:T(512)}, u32[]{:S(2)}) copy-start(f32[320]{0:T(512)} %add_multiply_fusion) | copy-start | bytes 3844
  401.3 6.3 %copy-start.2 = (bf16[1,1,2048,384]{2,3,1,0:T(8,128)(2,1)S(1)}, bf16[1,1,2048,384]{2,3,1,0:T(8,128)(2,1)}, u32[]{:S(2)}) copy-start(bf16[1,1,2048,384]{2,3,1,0:T(8,128)(2,1)} %copy.273) | copy-start | bytes 4718596
  401.4 6.3 %copy-start.5 = (f32[320,384]{0,1:T(8,128)S(1)}, f32[320,384]{0,1:T(8,128)}, u32[]{:S(2)}) copy-start(f32[320,384]{0,1:T(8,128)} %copy.242) | copy-start | bytes 1474564
  401.4 6.3 %copy-start.14 = (pred[320,2048]{1,0:T(8,128)(4,1)S(1)}, pred[320,2048]{1,0:T(8,128)(4,1)}, u32[]{:S(2)}) copy-start(pred[320,2048]{1,0:T(8,128)(4,1)} %get-tuple-element.49) | copy-start | bytes 1966084
  401.4 6.3 %copy-start.20 = (f32[320]{0:T(512)S(1)}, f32[320]{0:T(512)}, u32[]{:S(2)}) copy-start(f32[320]{0:T(512)} %copy-done.19) | copy-start | bytes 3844
  401.4 6.3 %copy-start.26 = (f32[384]{0:T(512)S(1)}, f32[384]{0:T(512)}, u32[]{:S(2)}) copy-start(f32[384]{0:T(512)} %copy-done.25) | copy-start | bytes 4612
  406.7 38.8 %collective-permute-start.15 = (bf16[320,1280]{1,0:T(8,128)(2,1)}, bf16[320,1280]{1,0:T(8,128)(2,1)}, u32[]{:S(2)}, u32[]{:S(2)}) collective-permute-start(bf16[320,1280]{1,0:T(8,128)(2,1)} %convolution_convert_fusion.3), channel_id=1, source_target_pairs={{0,1},{1,0},{2,3},{3,2},{4,5},{5,4},{6,7},{7,6},{8,9},{9,8},{10,11... | collective-permute-start | bytes 2457608 | tf_op jit(solution)/shard_map/ppermute | solution.py:20
  437.9 12.7 %collective-permute-start.17 = (bf16[320,1280]{1,0:T(8,128)(2,1)}, bf16[320,1280]{1,0:T(8,128)(2,1)}, u32[]{:S(2)}, u32[]{:S(2)}) collective-permute-start(bf16[320,1280]{1,0:T(8,128)(2,1)} %convolution_convert_fusion), channel_id=1, source_target_pairs={{0,1},{1,0},{2,3},{3,2},{4,5},{5,4},{6,7},{7,6},{8,9},{9,8},{10,11... | collective-permute-start | bytes 2457608 | tf_op jit(solution)/shard_map/ppermute | solution.py:20
  453.6 23.6 %copy-start.4 = (bf16[5120,64]{0,1:T(8,128)(2,1)S(1)}, bf16[5120,64]{0,1:T(8,128)(2,1)}, u32[]{:S(2)}) copy-start(bf16[5120,64]{0,1:T(8,128)(2,1)} %param.32) | copy-start | bytes 1966084
  454.9 9.3 %all-to-all-start.9 = ((f32[4,80,66]{1,2,0:T(8,128)}), f32[4,80,66]{1,2,0:T(8,128)S(1)}, u32[]{:S(2)}, u32[]{:S(2)}) async-start(f32[4,80,66]{1,2,0:T(8,128)} %pad_maximum_fusion.5), calls=%async_computation.10 | async-start | bytes 294912 | tf_op jit(solution)/shard_map/all_to_all | solution.py:108
  458.3 35.2 %copy-start.17 = (f32[160,32]{0,1:T(8,128)S(1)}, f32[160,32]{0,1:T(8,128)}, u32[]{:S(2)}) copy-start(f32[160,32]{0,1:T(8,128)} %param.21) | copy-start | bytes 61444
  464.2 9.5 %all-to-all-start.10 = ((f32[4,80,66]{1,2,0:T(8,128)}), f32[4,80,66]{1,2,0:T(8,128)S(1)}, u32[]{:S(2)}, u32[]{:S(2)}) async-start(f32[4,80,66]{1,2,0:T(8,128)} %pad_maximum_fusion.6), calls=%async_computation.11 | async-start | bytes 294912 | tf_op jit(solution)/shard_map/all_to_all | solution.py:108
  473.7 14.7 %all-to-all-start.5 = ((bf16[4,80,640]{2,1,0:T(8,128)(2,1)}), bf16[4,80,640]{2,1,0:T(8,128)(2,1)S(1)}, u32[]{:S(2)}, u32[]{:S(2)}) async-start(bf16[4,80,640]{2,1,0:T(8,128)(2,1)} %constant_dynamic-slice_fusion.1), calls=%async_computation.6 | async-start | bytes 819200 | tf_op jit(solution)/shard_map/all_to_all | solution.py:260
  488.4 12.5 %all-to-all-start.8 = ((bf16[4,80,640]{2,1,0:T(8,128)(2,1)}), bf16[4,80,640]{2,1,0:T(8,128)(2,1)S(1)}, u32[]{:S(2)}, u32[]{:S(2)}) async-start(bf16[4,80,640]{2,1,0:T(8,128)(2,1)} %constant_dynamic-slice_fusion), calls=%async_computation.9 | async-start | bytes 819200 | tf_op jit(solution)/shard_map/all_to_all | solution.py:260
  492.1 1.3 collective-permute-start.18
  (18 other events, 74.9 us)
Sparse Core Ops, SparseCore 0:
  89.5 107.7 reduce-scatter.1

commit v3 on v2

--- a/solution.py
+++ b/solution.py
@@ -123,7 +123,13 @@
             return terms.astype(F32) + flip(terms, "wt").astype(F32)
         return lax.psum(terms, "wt").astype(F32)
 
-    wide_query, wide_key, wide_value = wide(w_query), wide(w_key), wide(w_value)
+    if paired:
+        key_pair = ordered(w_key, flip(w_key, "t"), t_index)
+        key_pair, w_query, w_value = lax.optimization_barrier((key_pair, w_query, w_value))
+        wide_key = ordered(key_pair, flip(key_pair, "cfg"), half_index)
+    else:
+        wide_key = wide(w_key)
+    wide_query, wide_value = wide(w_query), wide(w_value)
     wide_out, wide_cross, wide_cross_out = wide(w_out), wide(w_cross_query), wide(w_cross_out)
 
     chunks = CHUNKS if groups > 1 and tok % (CHUNKS * 16) == 0 else 1
@@ -133,6 +139,11 @@
     def by_chunk(x):
         shape = (groups, chunks, part) + x.shape[2:]
         return jnp.swapaxes(x.reshape(shape), 0, 1).reshape((rows,) + x.shape[2:])
+
+    def three_terms(x):
+        high = lax.reduce_precision(x, 8, 7)
+        middle = lax.reduce_precision(x - high, 8, 7)
+        return [term.astype(BF) for term in (high, middle, x - high - middle)]
 
     own = hidden[0].astype(F32)
     mean = jnp.mean(own, axis=-1, keepdims=True)
@@ -143,10 +154,7 @@
     if groups == 1:
         sliced = own
     else:
-        high = lax.reduce_precision(facts, 8, 7)
-        middle = lax.reduce_precision(facts - high, 8, 7)
-        low = facts - high - middle
-        extra = jnp.concatenate([high, middle, low], axis=1).astype(BF)
+        extra = jnp.concatenate(three_terms(facts), axis=1)
         extra = jnp.pad(extra, ((0, 0), (0, 128 - extra.shape[1])))
         features = hidden[0].reshape(tok, halves, groups, slice_width // halves)
         features = jnp.concatenate(
@@ -212,7 +220,8 @@
         )
 
     column_sums = jnp.dot(jnp.ones((8, slice_width), BF), wide_cross, preferred_element_type=F32)
-    column_sums = sum_at_owner(column_sums[0].reshape(groups, 1, my_cols))
+    column_sums = column_sums[0].reshape(groups, 1, my_cols)
+    riding = groups > 1 and chunk_rows <= my_cols
 
     text = lax.dynamic_slice_in_dim(text_kv[:, 0], z_index * my_cols, my_cols, 2)
     text_keys = text[0].reshape(-1, heads, HD).astype(F32)
@@ -229,11 +238,25 @@
         shifted = (sliced[i] - facts[i, 0:1]) + both_columns(project_out(block_mixed, wide_out))
         states.append(shifted)
         sums = jnp.stack([jnp.sum(shifted, axis=1), jnp.sum(shifted * shifted, axis=1)])
-        sums = sum_at_owner(jnp.broadcast_to(sums[None], (groups,) + sums.shape)) / width
         crossed = jnp.dot(shifted.astype(BF), wide_cross, preferred_element_type=F32).astype(BF)
-        crossed = sum_at_owner(to_groups(crossed, my_cols))
+        crossed = to_groups(crossed, my_cols)
+        if riding:
+            sums = jnp.concatenate(three_terms(sums))
+            sums = jnp.pad(sums, ((0, 0), (0, my_cols - chunk_rows)))
+            sums = jnp.broadcast_to(sums[None], (groups,) + sums.shape)
+            below = jnp.concatenate([sums] + three_terms(column_sums), axis=1)
+            below = jnp.pad(below, ((0, 0), (0, 16 - below.shape[1]), (0, 0)))
+            arrived = sum_at_owner(jnp.concatenate([crossed, below], axis=1))
+            crossed, below = arrived[:chunk_rows], arrived[chunk_rows:]
+            sums = (below[0:2] + below[2:4] + below[4:6])[:, :chunk_rows]
+            all_columns = below[6:7] + below[7:8] + below[8:9]
+        else:
+            sums = sum_at_owner(jnp.broadcast_to(sums[None], (groups,) + sums.shape))
+            all_columns = sum_at_owner(column_sums)
+            crossed = sum_at_owner(crossed)
+        sums = sums / width
         variance = jnp.maximum(sums[1] - sums[0] * sums[0], 0.0)[:, None, None]
-        shaped = (crossed - sums[0][:, None] * column_sums).reshape(chunk_rows, heads, HD)
+        shaped = (crossed - sums[0][:, None] * all_columns).reshape(chunk_rows, heads, HD)
         square = jnp.mean(shaped * shaped, axis=-1, keepdims=True)
         cross_queries = (shaped * lax.rsqrt(square + EPS * (variance + EPS))).astype(BF)
         allowed = (my_tenant[i][:, None] == text_tenant[None, :]) & live[None]
@@ -246,27 +269,15 @@
     totals = jnp.sum(w_head.astype(F32), axis=0)[None]
     out_width = width // columns
 
-    leaving, velocity = [], []
+    leaving, sums = [], []
     for i, shifted, block_mixed in zip(spans, states, cross_mixed):
         shifted = shifted + both_columns(project_out(block_mixed, wide_cross_out))
         final = (shifted + facts[i, 0:1]).astype(BF)
-        if groups == 1:
-            leaving.append(lax.dynamic_slice_in_dim(final, wt_index * out_width, out_width, 1))
-        else:
-            final = final.reshape(groups, part, slice_width)
-            if columns == halves:
-                span = slice_width // halves
-                final = lax.dynamic_slice_in_dim(final, wt_index * span, span, 2)
-            final = jnp.swapaxes(lax.all_to_all(final, "z", 0, 0), 0, 1)
-            if columns == halves:
-                leaving.append(final.reshape(part, out_width))
-            else:
-                final = final.reshape(part, groups, halves, -1)
-                final = jnp.swapaxes(final, 1, 2).reshape(part, width)
-                leaving.append(
-                    lax.dynamic_slice_in_dim(final, wt_index * out_width, out_width, 1)
-                )
-        sums = jnp.concatenate(
+        if groups > 1 and columns == halves:
+            span = slice_width // halves
+            final = lax.dynamic_slice_in_dim(final, wt_index * span, span, 1)
+        leaving.append(final.reshape(groups, part, -1))
+        some = jnp.concatenate(
             [
                 jnp.dot(shifted.astype(BF), head_rows, preferred_element_type=F32),
                 jnp.sum(shifted, axis=1, keepdims=True),
@@ -274,12 +285,24 @@
             ],
             axis=1,
         )
-        sums = sum_at_owner(sums.reshape(groups, part, channels + 2))
-        mean = sums[:, channels : channels + 1] / width
-        variance = jnp.maximum(sums[:, channels + 1 :] / width - mean * mean, 0.0)
-        velocity.append((sums[:, :channels] - mean * totals) * lax.rsqrt(variance + EPS))
-    hidden_out = jnp.concatenate(leaving)
-    velocity = jnp.concatenate(velocity)
+        sums.append(some.reshape(groups, part, channels + 2))
+    sums = sum_at_owner(jnp.concatenate(sums, axis=1))
+    mean = sums[:, channels : channels + 1] / width
+    variance = jnp.maximum(sums[:, channels + 1 :] / width - mean * mean, 0.0)
+    velocity = (sums[:, :channels] - mean * totals) * lax.rsqrt(variance + EPS)
+
+    leaving = jnp.concatenate(leaving, axis=1)
+    if groups == 1:
+        hidden_out = lax.dynamic_slice_in_dim(leaving[0], wt_index * out_width, out_width, 1)
+    else:
+        leaving = jnp.swapaxes(lax.all_to_all(leaving, "z", 0, 0), 0, 1)
+        if columns == halves:
+            hidden_out = leaving.reshape(tok, out_width)
+        else:
+            leaving = jnp.swapaxes(leaving.reshape(tok, groups, halves, -1), 1, 2)
+            hidden_out = lax.dynamic_slice_in_dim(
+                leaving.reshape(tok, width), wt_index * out_width, out_width, 1
+            )
 
     channel_half = latent.shape[1]
     outgoing = lax.dynamic_slice_in_dim(velocity, (1 - half_index) * channel_half, channel_half, 1)

time: 514 us -> 494 us (0.961)
  starting transfers between devices: 62.1 us -> 44 us
  local copies, waits for them, and re-layouts: 46.7 us -> 35.7 us
  waiting for transfers between devices: 181 us -> 172 us
  matrix products: 72.1 us -> 79.2 us
  blocking collectives: 75 us -> 80.8 us
    all_to_all x8 -> x4, waiting for transfers between devices: 111 us -> 94.8 us  [sum_at_owner(): return jnp.sum(lax.all_to_all(x, 'z', 0, 0).astype(F32), axis=0)]
    all_to_all x8 -> x4, starting transfers between devices: 32.7 us -> 18 us  [sum_at_owner(): return jnp.sum(lax.all_to_all(x, 'z', 0, 0).astype(F32), axis=0)]
    ppermute x19, waiting for transfers between devices: 53.3 us -> 67.1 us  [flip(): return lax.ppermute(block, axis, [(0, 1), (1, 0)])]
    all_to_all x2 -> x1, waiting for transfers between devices: 16.9 us -> 10.1 us  [on_device(): leaving = jnp.swapaxes(lax.all_to_all(leaving, 'z', 0, 0), 0, 1)]
    all_gather x4, blocking collectives: 75 us -> 80.8 us  [join_groups(): x = lax.all_gather(x, 'z', axis=0)]
  transfers between devices with their start and end apart: 31 -> 26, of which waited for: 15 -> 12; matrix products, arithmetic and copies ran while one was open for 30% -> 31% of each run, Pallas kernels for 0% -> 0%
where the time goes in v3:
time: 494 us; the launch traced here: 489 us
  waiting for transfers between devices  172 us (35%)
  blocking collectives  80.8 us (16%)
  matrix products  79.2 us (16%)
  other arithmetic  60.3 us (12%)
  starting transfers between devices  44 us (9%)
  local copies, waits for them, and re-layouts  35.7 us (7%)
  between operations  16.5 us (3%)
    all_to_all x4, waiting for transfers between devices, sum_at_owner(): return jnp.sum(lax.all_to_all(x, 'z', 0, 0).astype(F32), axis=0)  94.8 us
    all_gather x4, blocking collectives, join_groups(): x = lax.all_gather(x, 'z', axis=0)  80.8 us
    ppermute x19, waiting for transfers between devices, flip(): return lax.ppermute(block, axis, [(0, 1), (1, 0)])  67.1 us
    select_n x6, other arithmetic, ordered(): jnp.where(index == 0, jnp.concatenate([mine, other]), jnp.concatenate([ot...  22.6 us
    dot_general x4, matrix products, project_out(): lax.dot_general(join_groups(mixed), weight, (((1,), (1,)), ((), ())), pre...  21.2 us
    all_to_all x4, starting transfers between devices, sum_at_owner(): return jnp.sum(lax.all_to_all(x, 'z', 0, 0).astype(F32), axis=0)  18 us
    dot_general x3, matrix products, project(): jnp.dot(normed, w, preferred_element_type=F32).astype(BF)  17.4 us
    ppermute x19, starting transfers between devices, flip(): return lax.ppermute(block, axis, [(0, 1), (1, 0)])  16.9 us
  transfers between devices with their start and end apart: 26, of which 12 were waited for; matrix products, arithmetic and copies ran while one was open for 31% of the time, Pallas kernels for 0%

profile of v3, /device:TPU:0, one launch (start us, length us, event | category | flops | bytes accessed | tf_op | source)
XLA Modules:
  0.0 488.6 jit_solution(2260151145108488549)
XLA Ops:
  7.2 3.0 collective-permute-start
  11.9 3.3 reshape_squeeze.10
  19.0 4.9 all-to-all-start
  24.5 7.8 %collective-permute-done = bf16[320,1536]{1,0:T(8,128)(2,1)} collective-permute-done((bf16[320,1536]{1,0:T(8,128)(2,1)}, bf16[320,1536]{1,0:T(8,128)(2,1)}, u32[]{:S(2)}, u32[]{:S(2)}) %collective-permute-start) | collective-permute-done | bytes 983072 | tf_op jit(solution)/shard_map/ppermute | solution.py:20
  32.3 3.4 maximum_select_fusion.15
  37.7 23.0 %collective-permute-done.1 = bf16[320,1536]{1,0:T(8,128)(2,1)} collective-permute-done((bf16[320,1536]{1,0:T(8,128)(2,1)}, bf16[320,1536]{1,0:T(8,128)(2,1)}, u32[]{:S(2)}, u32[]{:S(2)}) %collective-permute-start.1) | collective-permute-done | bytes 983072 | tf_op jit(solution)/shard_map/ppermute | solution.py:20
  60.7 4.0 maximum_select_fusion.16
  64.7 15.2 %collective-permute-done.3 = bf16[320,1536]{1,0:T(8,128)(2,1)S(1)} collective-permute-done((bf16[320,1536]{1,0:T(8,128)(2,1)}, bf16[320,1536]{1,0:T(8,128)(2,1)S(1)}, u32[]{:S(2)}, u32[]{:S(2)}) %collective-permute-start.3) | collective-permute-done | bytes 983072 | tf_op jit(solution)/shard_map/ppermute | solution.py:20
  79.9 3.4 maximum_select_fusion.17
  85.6 6.7 %fusion.28 = bf16[640,1536]{1,0:T(8,128)(2,1)S(1)} fusion(bf16[640,1280]{1,0:T(8,128)(2,1)S(1)} %fusion.25, bf16[640,1536]{1,0:T(8,128)(2,1)} %collective-permute-done.2, bf16[640,1536]{1,0:T(8,128)(2,1)} %maximum_select_fusion.16, pred[]{:T(512)S(6)} %eq.50), kind=kOutput, calls=%fused_computation.49 | convolution fusion | flops 2535260160 | bytes 7536641 | tf_op jit(solution)/shard_map/dot_general | solution.py:173
  92.6 6.2 %fusion.27 = bf16[640,1536]{1,0:T(8,128)(2,1)S(1)} fusion(bf16[640,1280]{1,0:T(8,128)(2,1)S(1)} %fusion.25, bf16[640,1536]{1,0:T(8,128)(2,1)} %collective-permute-done.4, bf16[640,1536]{1,0:T(8,128)(2,1)} %maximum_select_fusion.17, pred[]{:T(512)S(6)} %eq.50), kind=kOutput, calls=%fused_computation.48 | convolution fusion | flops 2535260160 | bytes 7536641 | tf_op jit(solution)/shard_map/dot_general | solution.py:173
  103.2 3.6 collective-permute-done.6
  106.8 4.5 fusion.26
  112.8 5.0 %all-to-all-start.1 = ((bf16[4,640,384]{2,1,0:T(8,128)(2,1)}), bf16[4,640,384]{2,1,0:T(8,128)(2,1)S(1)}, u32[]{:S(2)}, u32[]{:S(2)}) async-start(bf16[4,640,384]{2,1,0:T(8,128)(2,1)} %bitcast.160), calls=%async_computation.2 | async-start | bytes 3932160 | tf_op jit(solution)/shard_map/all_to_all | solution.py:108
  121.9 3.9 constant_dynamic-slice_fusion.2
  125.8 2.7 copy.262
  133.2 78.5 %all-to-all-done.1 = bf16[4,640,384]{2,1,0:T(8,128)(2,1)S(1)} async-done(((bf16[4,640,384]{2,1,0:T(8,128)(2,1)}), bf16[4,640,384]{2,1,0:T(8,128)(2,1)S(1)}, u32[]{:S(2)}, u32[]{:S(2)}) %all-to-all-start.1) | async-done | bytes 1966112 | tf_op jit(solution)/shard_map/all_to_all | solution.py:108
  215.5 4.0 maximum_select_fusion.18
  219.5 3.9 maximum_select_fusion.19
  230.9 4.0 convert_reduce_fusion.2
  234.9 2.9 convert_reduce_fusion.3
  241.3 2.5 fusion.49
  244.2 20.4 %all_gather.14 = bf16[4,320,384]{2,1,0:T(8,128)(2,1)S(1)} all-gather(bf16[1,320,384]{2,1,0:T(8,128)(2,1)S(1)} %copy.230), channel_id=1, replica_groups=mesh['cfg'=2,'z'=4,'t'=2,'wt'=2] {'z'}, dimensions={0}, use_global_device_ids=true | all-gather | bytes 1228800 | tf_op jit(solution)/shard_map/all_gather | solution.py:102
  264.8 4.4 convolution_convert_fusion.2
  272.2 18.6 %all_gather.12 = bf16[4,320,384]{2,1,0:T(8,128)(2,1)S(1)} all-gather(bf16[1,320,384]{2,1,0:T(8,128)(2,1)S(1)} %copy.214), channel_id=1, replica_groups=mesh['cfg'=2,'z'=4,'t'=2,'wt'=2] {'z'}, dimensions={0}, use_global_device_ids=true | all-gather | bytes 1228800 | tf_op jit(solution)/shard_map/all_gather | solution.py:102
  291.0 5.3 %convolution_convert_fusion.5 = bf16[320,1280]{1,0:T(8,128)(2,1)} fusion(bf16[320,1536]{1,0:T(8,128)(2,1)S(1)} %bitcast.200, bf16[640,1536]{1,0:T(8,128)(2,1)} %collective-permute-done.9, bf16[640,1536]{1,0:T(8,128)(2,1)} %maximum_select_fusion.18, pred[]{:T(512)S(6)} %eq.50), kind=kOutput, calls=%fused_computation.57 | convolution fusion | flops 1276395520 | bytes 5734401 | tf_op jit(solution)/shard_map/dot_general | solution.py:218
  298.6 4.6 convolution_reduce_fusion
  303.3 5.7 %collective-permute-done.10 = bf16[320,1280]{1,0:T(8,128)(2,1)} collective-permute-done((bf16[320,1280]{1,0:T(8,128)(2,1)}, bf16[320,1280]{1,0:T(8,128)(2,1)}, u32[]{:S(2)}, u32[]{:S(2)}) %collective-permute-start.10) | collective-permute-done | bytes 819232 | tf_op jit(solution)/shard_map/ppermute | solution.py:20
  308.9 3.8 fusion.106
  312.9 5.3 %convolution_convert_fusion.4 = bf16[320,1536]{1,0:T(8,128)(2,1)S(1)} fusion(f32[320,1280]{1,0:T(8,128)S(1)} %get-tuple-element.33, bf16[640,1536]{1,0:T(8,128)(2,1)} %collective-permute-done.12, bf16[640,1536]{1,0:T(8,128)(2,1)} %maximum_select_fusion.19, pred[]{:T(512)S(6)} %eq.50), kind=kOutput, calls=%fused_computation.56 | convolution fusion | flops 1276887040 | bytes 6553601 | tf_op jit(solution)/shard_map/dot_general | solution.py:241
  319.5 4.3 all-to-all-start.2
  325.7 3.9 maximum_select_fusion.20
  329.7 5.0 %convolution_convert_fusion.1 = bf16[320,1536]{1,0:T(8,128)(2,1)S(1)} fusion(f32[320,1280]{1,0:T(8,128)S(1)} %get-tuple-element.39, bf16[640,1536]{1,0:T(8,128)(2,1)} %collective-permute-done.12, bf16[640,1536]{1,0:T(8,128)(2,1)} %maximum_select_fusion.19, pred[]{:T(512)S(6)} %eq.50), kind=kOutput, calls=%fused_computation.53 | convolution fusion | flops 1276887040 | bytes 6553601 | tf_op jit(solution)/shard_map/dot_general | solution.py:241
  335.9 5.8 %all-to-all-done.2 = bf16[4,336,384]{2,1,0:T(8,128)(2,1)} async-done(((bf16[4,336,384]{2,1,0:T(8,128)(2,1)}), bf16[4,336,384]{2,1,0:T(8,128)(2,1)}, u32[]{:S(2)}, u32[]{:S(2)}) %all-to-all-start.2) | async-done | bytes 1032224 | tf_op jit(solution)/shard_map/all_to_all | solution.py:108
  341.7 4.6 all-to-all-start.3
  352.0 4.1 convert_reduce_fusion.1
  360.1 25.3 %all_gather.13 = bf16[4,320,384]{2,1,0:T(8,128)(2,1)S(1)} all-gather(bf16[1,320,384]{2,1,0:T(8,128)(2,1)} %copy.226), channel_id=1, replica_groups=mesh['cfg'=2,'z'=4,'t'=2,'wt'=2] {'z'}, dimensions={0}, use_global_device_ids=true | all-gather | bytes 1228800 | tf_op jit(solution)/shard_map/all_gather | solution.py:102
  387.9 6.0 %convolution_convert_fusion.3 = bf16[320,1280]{1,0:T(8,128)(2,1)} fusion(bf16[320,1536]{1,0:T(8,128)(2,1)} %bitcast.197, bf16[640,1536]{1,0:T(8,128)(2,1)} %collective-permute-done.14, bf16[640,1536]{1,0:T(8,128)(2,1)} %maximum_select_fusion.20, pred[]{:T(512)S(6)} %eq.50), kind=kOutput, calls=%fused_computation.55 | convolution fusion | flops 1276395520 | bytes 5734401 | tf_op jit(solution)/shard_map/dot_general | solution.py:218
  398.5 4.1 convert_reduce_fusion
  404.3 16.5 %all_gather.15 = bf16[4,320,384]{2,1,0:T(8,128)(2,1)S(1)} all-gather(bf16[1,320,384]{2,1,0:T(8,128)(2,1)S(1)} %copy.241), channel_id=1, replica_groups=mesh['cfg'=2,'z'=4,'t'=2,'wt'=2] {'z'}, dimensions={0}, use_global_device_ids=true | all-gather | bytes 1228800 | tf_op jit(solution)/shard_map/all_gather | solution.py:102
  420.9 5.5 %convolution_convert_fusion = bf16[320,1280]{1,0:T(8,128)(2,1)} fusion(bf16[320,1536]{1,0:T(8,128)(2,1)S(1)} %bitcast.201, bf16[640,1536]{1,0:T(8,128)(2,1)} %collective-permute-done.14, bf16[640,1536]{1,0:T(8,128)(2,1)} %maximum_select_fusion.20, pred[]{:T(512)S(6)} %eq.50), kind=kOutput, calls=%fused_computation.52 | convolution fusion | flops 1276395520 | bytes 5734401 | tf_op jit(solution)/shard_map/dot_general | solution.py:218
  429.7 2.6 fusion.108
  432.2 6.8 %collective-permute-done.17 = bf16[320,1280]{1,0:T(8,128)(2,1)} collective-permute-done((bf16[320,1280]{1,0:T(8,128)(2,1)}, bf16[320,1280]{1,0:T(8,128)(2,1)}, u32[]{:S(2)}, u32[]{:S(2)}) %collective-permute-start.17) | collective-permute-done | bytes 819232 | tf_op jit(solution)/shard_map/ppermute | solution.py:20
  439.0 3.0 fusion.109
  447.0 4.1 all-to-all-start.5
  452.2 10.6 %all-to-all-done.5 = f32[4,160,66]{1,2,0:T(8,128)} async-done(((f32[4,160,66]{1,2,0:T(8,128)}), f32[4,160,66]{1,2,0:T(8,128)}, u32[]{:S(2)}, u32[]{:S(2)}) %all-to-all-start.5) | async-done | bytes 168992 | tf_op jit(solution)/shard_map/all_to_all | solution.py:108
  462.8 3.7 all-to-all-start.4
  469.8 10.1 %all-to-all-done.4 = bf16[4,160,640]{2,1,0:T(8,128)(2,1)S(1)} async-done(((bf16[4,160,640]{2,1,0:T(8,128)(2,1)}), bf16[4,160,640]{2,1,0:T(8,128)(2,1)S(1)}, u32[]{:S(2)}, u32[]{:S(2)}) %all-to-all-start.4) | async-done | bytes 819232 | tf_op jit(solution)/shard_map/all_to_all | solution.py:298
  (215 shorter events, 81.6 us)
Async XLA Ops:
  7.2 8.1 %copy-start.1 = (bf16[1,160,5120]{2,1,0:T(8,128)(2,1)S(1)}, bf16[1,160,5120]{2,1,0:T(8,128)(2,1)}, u32[]{:S(2)}) copy-start(bf16[1,160,5120]{2,1,0:T(8,128)(2,1)} %param.20) | copy-start | bytes 4915204
  7.2 8.7 %copy-start.16 = (s32[160,3]{0,1:T(4,128)S(1)}, s32[160,3]{0,1:T(4,128)}, u32[]{:S(2)}) copy-start(s32[160,3]{0,1:T(4,128)} %param.23) | copy-start | bytes 5764
  7.2 25.1 %collective-permute-start = (bf16[320,1536]{1,0:T(8,128)(2,1)}, bf16[320,1536]{1,0:T(8,128)(2,1)}, u32[]{:S(2)}, u32[]{:S(2)}) collective-permute-start(bf16[320,1536]{1,0:T(8,128)(2,1)} %param.27), channel_id=1, source_target_pairs={{0,2},{2,0},{1,3},{3,1},{4,6},{6,4},{5,7},{7,5},{8,10},{10,8},{9,1... | collective-permute-start | bytes 2949128 | tf_op jit(solution)/shard_map/ppermute | solution.py:20
  17.6 14.7 %copy-start.11 = (bf16[320,1536]{1,0:T(8,128)(2,1)S(1)}, bf16[320,1536]{1,0:T(8,128)(2,1)}, u32[]{:S(2)}) copy-start(bf16[320,1536]{1,0:T(8,128)(2,1)} %param.27) | copy-start | bytes 2949124
  19.0 64.3 %all-to-all-start = ((bf16[4,160,1408]{2,1,0:T(8,128)(2,1)}), bf16[4,160,1408]{2,1,0:T(8,128)(2,1)S(1)}, u32[]{:S(2)}, u32[]{:S(2)}) async-start(bf16[4,160,1408]{2,1,0:T(8,128)(2,1)} %copy.195), calls=%async_computation | async-start | bytes 3604480 | tf_op jit(solution)/shard_map/all_to_all | solution.py:165
  23.9 202.7 %reduce-scatter.2.cloned.1.call-start = ((), (), s32[]{:S(2)}) async-start(), calls=%async_computation.7 | async-start | bytes 4915200 | tf_op jit(solution)/shard_map/reduce_scatter | solution.py:113
  35.7 25.0 %collective-permute-start.1 = (bf16[320,1536]{1,0:T(8,128)(2,1)}, bf16[320,1536]{1,0:T(8,128)(2,1)}, u32[]{:S(2)}, u32[]{:S(2)}) collective-permute-start(bf16[320,1536]{1,0:T(8,128)(2,1)} %param.26), channel_id=1, source_target_pairs={{0,2},{2,0},{1,3},{3,1},{4,6},{6,4},{5,7},{7,5},{8,10},{10,8},{9,1... | collective-permute-start | bytes 2949128 | tf_op jit(solution)/shard_map/ppermute | solution.py:20
  37.4 42.5 %collective-permute-start.3 = (bf16[320,1536]{1,0:T(8,128)(2,1)}, bf16[320,1536]{1,0:T(8,128)(2,1)S(1)}, u32[]{:S(2)}, u32[]{:S(2)}) collective-permute-start(bf16[320,1536]{1,0:T(8,128)(2,1)} %param.28), channel_id=1, source_target_pairs={{0,2},{2,0},{1,3},{3,1},{4,6},{6,4},{5,7},{7,5},{8,10},{10,8},{9,1... | collective-permute-start | bytes 2949128 | tf_op jit(solution)/shard_map/ppermute | solution.py:20
  64.7 21.0 %collective-permute-start.2 = (bf16[640,1536]{1,0:T(8,128)(2,1)}, bf16[640,1536]{1,0:T(8,128)(2,1)}, u32[]{:S(2)}, u32[]{:S(2)}) collective-permute-start(bf16[640,1536]{1,0:T(8,128)(2,1)} %maximum_select_fusion.16), channel_id=1, source_target_pairs={{0,16},{16,0},{1,17},{17,1},{2,18},{18,2},{3,19},{19,3},{4,20},{20... | collective-permute-start | bytes 5898248 | tf_op jit(solution)/shard_map/ppermute | solution.py:20
  83.3 9.2 %collective-permute-start.4 = (bf16[640,1536]{1,0:T(8,128)(2,1)}, bf16[640,1536]{1,0:T(8,128)(2,1)}, u32[]{:S(2)}, u32[]{:S(2)}) collective-permute-start(bf16[640,1536]{1,0:T(8,128)(2,1)} %maximum_select_fusion.17), channel_id=1, source_target_pairs={{0,16},{16,0},{1,17},{17,1},{2,18},{18,2},{3,19},{19,3},{4,20},{20... | collective-permute-start | bytes 5898248 | tf_op jit(solution)/shard_map/ppermute | solution.py:20
  83.8 1.8 copy-start
  85.6 6.9 %copy-start.8 = (bf16[640,1280]{1,0:T(8,128)(2,1)}, bf16[640,1280]{1,0:T(8,128)(2,1)S(1)}, u32[]{:S(2)}) copy-start(bf16[640,1280]{1,0:T(8,128)(2,1)S(1)} %fusion.25) | copy-start | bytes 4915204
  102.7 4.1 collective-permute-start.6
  111.3 10.4 %copy-start.21 = (s32[4]{0:T(128)S(1)}, s32[4]{0:T(128)}, u32[]{:S(2)}) copy-start(s32[4]{0:T(128)} %param.22) | copy-start | bytes 52
  112.8 98.8 %all-to-all-start.1 = ((bf16[4,640,384]{2,1,0:T(8,128)(2,1)}), bf16[4,640,384]{2,1,0:T(8,128)(2,1)S(1)}, u32[]{:S(2)}, u32[]{:S(2)}) async-start(bf16[4,640,384]{2,1,0:T(8,128)(2,1)} %bitcast.160), calls=%async_computation.2 | async-start | bytes 3932160 | tf_op jit(solution)/shard_map/all_to_all | solution.py:108
  117.8 97.6 %collective-permute-start.8 = (bf16[320,1536]{1,0:T(8,128)(2,1)}, bf16[320,1536]{1,0:T(8,128)(2,1)}, u32[]{:S(2)}, u32[]{:S(2)}) collective-permute-start(bf16[320,1536]{1,0:T(8,128)(2,1)} %param.29), channel_id=1, source_target_pairs={{0,2},{2,0},{1,3},{3,1},{4,6},{6,4},{5,7},{7,5},{8,10},{10,8},{9,1... | collective-permute-start | bytes 2949128 | tf_op jit(solution)/shard_map/ppermute | solution.py:20
  119.4 100.1 %collective-permute-start.11 = (bf16[320,1536]{1,0:T(8,128)(2,1)}, bf16[320,1536]{1,0:T(8,128)(2,1)}, u32[]{:S(2)}, u32[]{:S(2)}) collective-permute-start(bf16[320,1536]{1,0:T(8,128)(2,1)} %param.30), channel_id=1, source_target_pairs={{0,2},{2,0},{1,3},{3,1},{4,6},{6,4},{5,7},{7,5},{8,10},{10,8},{9,1... | collective-permute-start | bytes 2949128 | tf_op jit(solution)/shard_map/ppermute | solution.py:20
  119.9 205.8 %collective-permute-start.13 = (bf16[320,1536]{1,0:T(8,128)(2,1)}, bf16[320,1536]{1,0:T(8,128)(2,1)}, u32[]{:S(2)}, u32[]{:S(2)}) collective-permute-start(bf16[320,1536]{1,0:T(8,128)(2,1)} %param.31), channel_id=1, source_target_pairs={{0,2},{2,0},{1,3},{3,1},{4,6},{6,4},{5,7},{7,5},{8,10},{10,8},{9,1... | collective-permute-start | bytes 2949128 | tf_op jit(solution)/shard_map/ppermute | solution.py:20
  125.8 6.1 %copy-start.20 = (s32[1,4]{1,0:T(1,128)S(1)}, s32[1,4]{1,0:T(1,128)}, u32[]{:S(2)}) copy-start(s32[1,4]{1,0:T(1,128)} %param.25) | copy-start | bytes 52
  125.8 6.2 %copy-start.17 = (f32[128]{0:T(128)S(1)}, f32[128]{0:T(128)}, u32[]{:S(2)}) copy-start(f32[128]{0:T(128)} %constant.137) | copy-start | bytes 1540
  125.8 6.2 %copy-start.18 = (f32[128]{0:T(128)S(1)}, f32[128]{0:T(128)}, u32[]{:S(2)}) copy-start(f32[128]{0:T(128)} %constant.138) | copy-start | bytes 1540
  125.8 6.2 %copy-start.19 = (f32[128]{0:T(128)S(1)}, f32[128]{0:T(128)}, u32[]{:S(2)}) copy-start(f32[128]{0:T(128)} %constant.139) | copy-start | bytes 1540
  130.4 82.8 %copy-start.14 = (bf16[128,128,1]{1,0,2:T(8,128)(2,1)S(1)}, bf16[128,128,1]{1,0,2:T(8,128)(2,1)}, u32[]{:S(2)}) copy-start(bf16[128,128,1]{1,0,2:T(8,128)(2,1)} %constant.140) | copy-start | bytes 98308
  213.9 12.4 %collective-permute-start.7 = (bf16[640,384]{0,1:T(8,128)(2,1)S(1)}, bf16[640,384]{0,1:T(8,128)(2,1)S(1)}, u32[]{:S(2)}, u32[]{:S(2)}) collective-permute-start(bf16[640,384]{0,1:T(8,128)(2,1)S(1)} %bitcast.204), channel_id=1, source_target_pairs={{0,2},{2,0},{1,3},{3,1},{4,6},{6,4},{5,7},{7,5},{8,10},{10,8},{9,1... | collective-permute-start | bytes 1474568 | tf_op jit(solution)/shard_map/ppermute | solution.py:20
  219.4 45.3 %collective-permute-start.9 = (bf16[640,1536]{1,0:T(8,128)(2,1)}, bf16[640,1536]{1,0:T(8,128)(2,1)}, u32[]{:S(2)}, u32[]{:S(2)}) collective-permute-start(bf16[640,1536]{1,0:T(8,128)(2,1)} %maximum_select_fusion.18), channel_id=1, source_target_pairs={{0,16},{16,0},{1,17},{17,1},{2,18},{18,2},{3,19},{19,3},{4,20},{20... | collective-permute-start | bytes 5898248 | tf_op jit(solution)/shard_map/ppermute | solution.py:20
  223.4 75.2 %collective-permute-start.12 = (bf16[640,1536]{1,0:T(8,128)(2,1)}, bf16[640,1536]{1,0:T(8,128)(2,1)}, u32[]{:S(2)}, u32[]{:S(2)}) collective-permute-start(bf16[640,1536]{1,0:T(8,128)(2,1)} %maximum_select_fusion.19), channel_id=1, source_target_pairs={{0,16},{16,0},{1,17},{17,1},{2,18},{18,2},{3,19},{19,3},{4,20},{20... | collective-permute-start | bytes 5898248 | tf_op jit(solution)/shard_map/ppermute | solution.py:20
  228.8 11.5 %collective-permute-start.5 = (bf16[640,384]{1,0:T(8,128)(2,1)S(1)}, bf16[640,384]{1,0:T(8,128)(2,1)S(1)}, u32[]{:S(2)}, u32[]{:S(2)}) collective-permute-start(bf16[640,384]{1,0:T(8,128)(2,1)S(1)} %get-tuple-element.43), channel_id=1, source_target_pairs={{0,2},{2,0},{1,3},{3,1},{4,6},{6,4},{5,7},{7,5},{8,10},{10,8},{9,1... | collective-permute-start | bytes 1474568 | tf_op jit(solution)/shard_map/ppermute | solution.py:20
  230.9 4.1 copy-start.13
  264.8 6.2 %copy-start.22 = (bf16[3,320,1280]{2,1,0:T(8,128)(2,1)S(1)}, bf16[3,320,1280]{2,1,0:T(8,128)(2,1)}, u32[]{:S(2)}) copy-start(bf16[3,320,1280]{2,1,0:T(8,128)(2,1)} %get-tuple-element.77) | copy-start | bytes 7372804
  269.2 3.0 copy-start.12
  269.2 34.0 %collective-permute-start.16 = (bf16[320,1280]{1,0:T(8,128)(2,1)S(1)}, bf16[320,1280]{1,0:T(8,128)(2,1)}, u32[]{:S(2)}, u32[]{:S(2)}) collective-permute-start(bf16[320,1280]{1,0:T(8,128)(2,1)S(1)} %convolution_convert_fusion.2), channel_id=1, source_target_pairs={{0,1},{1,0},{2,3},{3,2},{4,5},{5,4},{6,7},{7,6},{8,9},{9,8},{10,11... | collective-permute-start | bytes 2457608 | tf_op jit(solution)/shard_map/ppermute | solution.py:20
  291.0 5.7 %copy-start.4 = (bf16[1,1,2048,384]{3,2,1,0:T(8,128)(2,1)S(1)}, bf16[1,1,2048,384]{3,2,1,0:T(8,128)(2,1)}, u32[]{:S(2)}) copy-start(bf16[1,1,2048,384]{3,2,1,0:T(8,128)(2,1)} %get-tuple-element.36) | copy-start | bytes 4718596
  296.3 12.7 %collective-permute-start.10 = (bf16[320,1280]{1,0:T(8,128)(2,1)}, bf16[320,1280]{1,0:T(8,128)(2,1)}, u32[]{:S(2)}, u32[]{:S(2)}) collective-permute-start(bf16[320,1280]{1,0:T(8,128)(2,1)} %convolution_convert_fusion.5), channel_id=1, source_target_pairs={{0,1},{1,0},{2,3},{3,2},{4,5},{5,4},{6,7},{7,6},{8,9},{9,8},{10,11... | collective-permute-start | bytes 2457608 | tf_op jit(solution)/shard_map/ppermute | solution.py:20
  312.8 16.9 %copy-start.2 = (f32[320,1280]{1,0:T(8,128)}, f32[320,1280]{1,0:T(8,128)S(1)}, u32[]{:S(2)}) copy-start(f32[320,1280]{1,0:T(8,128)S(1)} %get-tuple-element.39) | copy-start | bytes 4915204
  319.5 22.2 %all-to-all-start.2 = ((bf16[4,336,384]{2,1,0:T(8,128)(2,1)}), bf16[4,336,384]{2,1,0:T(8,128)(2,1)}, u32[]{:S(2)}, u32[]{:S(2)}) async-start(bf16[4,336,384]{2,1,0:T(8,128)(2,1)} %fusion.51), calls=%async_computation.3 | async-start | bytes 2064384 | tf_op jit(solution)/shard_map/all_to_all | solution.py:108
  329.7 58.2 %collective-permute-start.14 = (bf16[640,1536]{1,0:T(8,128)(2,1)}, bf16[640,1536]{1,0:T(8,128)(2,1)}, u32[]{:S(2)}, u32[]{:S(2)}) collective-permute-start(bf16[640,1536]{1,0:T(8,128)(2,1)} %maximum_select_fusion.20), channel_id=1, source_target_pairs={{0,16},{16,0},{1,17},{17,1},{2,18},{18,2},{3,19},{19,3},{4,20},{20... | collective-permute-start | bytes 5898248 | tf_op jit(solution)/shard_map/ppermute | solution.py:20
  335.9 16.1 %copy-start.3 = (bf16[1,1,2048,384]{2,3,1,0:T(8,128)(2,1)S(1)}, bf16[1,1,2048,384]{2,3,1,0:T(8,128)(2,1)}, u32[]{:S(2)}) copy-start(bf16[1,1,2048,384]{2,3,1,0:T(8,128)(2,1)} %copy.262) | copy-start | bytes 4718596
  341.7 44.7 %all-to-all-start.3 = ((bf16[4,336,384]{2,1,0:T(8,128)(2,1)}), bf16[4,336,384]{2,1,0:T(8,128)(2,1)}, u32[]{:S(2)}, u32[]{:S(2)}) async-start(bf16[4,336,384]{2,1,0:T(8,128)(2,1)} %fusion.52), calls=%async_computation.4 | async-start | bytes 2064384 | tf_op jit(solution)/shard_map/all_to_all | solution.py:108
  352.0 4.2 copy-start.9
  393.9 35.8 %collective-permute-start.15 = (bf16[320,1280]{1,0:T(8,128)(2,1)}, bf16[320,1280]{1,0:T(8,128)(2,1)}, u32[]{:S(2)}, u32[]{:S(2)}) collective-permute-start(bf16[320,1280]{1,0:T(8,128)(2,1)} %convolution_convert_fusion.3), channel_id=1, source_target_pairs={{0,1},{1,0},{2,3},{3,2},{4,5},{5,4},{6,7},{7,6},{8,9},{9,8},{10,11... | collective-permute-start | bytes 2457608 | tf_op jit(solution)/shard_map/ppermute | solution.py:20
  398.5 4.2 copy-start.10
  420.9 7.0 %copy-start.5 = (bf16[5120,64]{0,1:T(8,128)(2,1)S(1)}, bf16[5120,64]{0,1:T(8,128)(2,1)}, u32[]{:S(2)}) copy-start(bf16[5120,64]{0,1:T(8,128)(2,1)} %param.32) | copy-start | bytes 1966084
  426.4 12.7 %collective-permute-start.17 = (bf16[320,1280]{1,0:T(8,128)(2,1)}, bf16[320,1280]{1,0:T(8,128)(2,1)}, u32[]{:S(2)}, u32[]{:S(2)}) collective-permute-start(bf16[320,1280]{1,0:T(8,128)(2,1)} %convolution_convert_fusion), channel_id=1, source_target_pairs={{0,1},{1,0},{2,3},{3,2},{4,5},{5,4},{6,7},{7,6},{8,9},{9,8},{10,11... | collective-permute-start | bytes 2457608 | tf_op jit(solution)/shard_map/ppermute | solution.py:20
  447.0 15.8 %all-to-all-start.5 = ((f32[4,160,66]{1,2,0:T(8,128)}), f32[4,160,66]{1,2,0:T(8,128)}, u32[]{:S(2)}, u32[]{:S(2)}) async-start(f32[4,160,66]{1,2,0:T(8,128)} %maximum_maximum_fusion), calls=%async_computation.6 | async-start | bytes 589824 | tf_op jit(solution)/shard_map/all_to_all | solution.py:108
  451.1 18.1 %copy-start.15 = (f32[160,32]{0,1:T(8,128)S(1)}, f32[160,32]{0,1:T(8,128)}, u32[]{:S(2)}) copy-start(f32[160,32]{0,1:T(8,128)} %param.21) | copy-start | bytes 61444
  451.3 15.2 %copy-start.6 = (bf16[5120,64]{0,1:T(8,128)(2,1)S(1)}, bf16[5120,64]{0,1:T(8,128)(2,1)}, u32[]{:S(2)}) copy-start(bf16[5120,64]{0,1:T(8,128)(2,1)} %param.32) | copy-start | bytes 1966084
  462.8 17.1 %all-to-all-start.4 = ((bf16[4,160,640]{2,1,0:T(8,128)(2,1)}), bf16[4,160,640]{2,1,0:T(8,128)(2,1)S(1)}, u32[]{:S(2)}, u32[]{:S(2)}) async-start(bf16[4,160,640]{2,1,0:T(8,128)(2,1)} %pad_maximum_fusion.3), calls=%async_computation.5 | async-start | bytes 1638400 | tf_op jit(solution)/shard_map/all_to_all | solution.py:298
  467.8 1.4 collective-permute-start.18
  (1 other events, 1.5 us)
Sparse Core Ops, SparseCore 0:
  101.3 107.5 reduce-scatter.1

commit v4 on v3

--- a/solution.py
+++ b/solution.py
@@ -169,11 +169,12 @@
         facts = extra[:, 0:5] + extra[:, 5:10] + extra[:, 10:15]
     normed = ((sliced - facts[:, 0:1]) * facts[:, 1:2]).astype(BF)
 
-    def project(w):
+    def project(normed, w):
         return to_groups(jnp.dot(normed, w, preferred_element_type=F32).astype(BF), my_cols)
 
-    projected_keys = sum_at_owner(project(wide_key)).astype(BF)
-    projected = jnp.concatenate([project(wide_query), project(wide_value)], axis=2)
+    projected_keys, normed = lax.optimization_barrier((project(normed, wide_key), normed))
+    projected_keys = sum_at_owner(projected_keys).astype(BF)
+    projected = jnp.concatenate([project(normed, wide_query), project(normed, wide_value)], axis=2)
     projected = sum_groups(projected.reshape(groups * rows, 2 * my_cols))
 
     table, swap = rotary_tables()
@@ -286,16 +287,26 @@
             axis=1,
         )
         sums.append(some.reshape(groups, part, channels + 2))
-    sums = sum_at_owner(jnp.concatenate(sums, axis=1))
+    sums = jnp.concatenate(sums, axis=1)
+    leaving = jnp.concatenate(leaving, axis=1)
+    if groups == 1:
+        sums = sums[0]
+    else:
+        facts_width = 3 * (channels + 2)
+        pad = -facts_width % 128
+        wide_row = leaving.shape[2]
+        leaving = jnp.concatenate([leaving] + three_terms(sums), axis=2)
+        leaving = lax.all_to_all(jnp.pad(leaving, ((0, 0), (0, 0), (0, pad))), "z", 0, 0)
+        sums = jnp.sum(leaving[:, :, wide_row:].astype(F32), axis=0)
+        sums = sum(sums[:, i * (channels + 2) : (i + 1) * (channels + 2)] for i in range(3))
+        leaving = jnp.swapaxes(leaving[:, :, :wide_row], 0, 1)
     mean = sums[:, channels : channels + 1] / width
     variance = jnp.maximum(sums[:, channels + 1 :] / width - mean * mean, 0.0)
     velocity = (sums[:, :channels] - mean * totals) * lax.rsqrt(variance + EPS)
 
-    leaving = jnp.concatenate(leaving, axis=1)
     if groups == 1:
         hidden_out = lax.dynamic_slice_in_dim(leaving[0], wt_index * out_width, out_width, 1)
     else:
-        leaving = jnp.swapaxes(lax.all_to_all(leaving, "z", 0, 0), 0, 1)
         if columns == halves:
             hidden_out = leaving.reshape(tok, out_width)
         else:

time: 494 us -> 495 us (level)
  starting transfers between devices: 44 us -> 38.4 us
  local copies, waits for them, and re-layouts: 35.7 us -> 41.1 us
  waiting for transfers between devices: 172 us -> 177 us
    all_to_all x1, waiting for transfers between devices: 10.1 us -> 20.1 us  [on_device(): lax.all_to_all(jnp.pad(leaving, ((0, 0), (0, 0), (0, pad))), 'z', 0, 0)]
    all_to_all x4 -> x3, waiting for transfers between devices: 94.8 us -> 90.3 us  [sum_at_owner(): return jnp.sum(lax.all_to_all(x, 'z', 0, 0).astype(F32), axis=0)]
    all_to_all x4 -> x3, starting transfers between devices: 18 us -> 13.9 us  [sum_at_owner(): return jnp.sum(lax.all_to_all(x, 'z', 0, 0).astype(F32), axis=0)]
  transfers between devices with their start and end apart: 26 -> 25, of which waited for: 12 -> 9; matrix products, arithmetic and copies ran while one was open for 31% -> 31% of each run, Pallas kernels for 0% -> 0%
where the time goes in v4:
time: 495 us; the launch traced here: 490 us
  waiting for transfers between devices  177 us (36%)
  blocking collectives  84.8 us (17%)
  matrix products  75.4 us (15%)
  other arithmetic  57.3 us (12%)
  local copies, waits for them, and re-layouts  41.1 us (8%)
  starting transfers between devices  38.4 us (8%)
  between operations  16.5 us (3%)
    all_to_all x3, waiting for transfers between devices, sum_at_owner(): return jnp.sum(lax.all_to_all(x, 'z', 0, 0).astype(F32), axis=0)  90.3 us
    all_gather x4, blocking collectives, join_groups(): x = lax.all_gather(x, 'z', axis=0)  84.8 us
    ppermute x19, waiting for transfers between devices, flip(): return lax.ppermute(block, axis, [(0, 1), (1, 0)])  66.2 us
    select_n x6, other arithmetic, ordered(): jnp.where(index == 0, jnp.concatenate([mine, other]), jnp.concatenate([ot...  22.5 us
    dot_general x4, matrix products, project_out(): lax.dot_general(join_groups(mixed), weight, (((1,), (1,)), ((), ())), pre...  21.1 us
    all_to_all x1, waiting for transfers between devices, on_device(): lax.all_to_all(jnp.pad(leaving, ((0, 0), (0, 0), (0, pad))), 'z', 0, 0)  20.1 us
    dot_general x3, matrix products, project(): jnp.dot(normed, w, preferred_element_type=F32).astype(BF)  17.2 us
    ppermute x19, starting transfers between devices, flip(): return lax.ppermute(block, axis, [(0, 1), (1, 0)])  15.4 us
  transfers between devices with their start and end apart: 25, of which 9 were waited for; matrix products, arithmetic and copies ran while one was open for 31% of the time, Pallas kernels for 0%

profile of v4, /device:TPU:0, one launch (start us, length us, event | category | flops | bytes accessed | tf_op | source)
XLA Modules:
  0.0 490.2 jit_solution(16320512848409007299)
XLA Ops:
  7.2 3.0 collective-permute-start
  17.0 5.0 %all-to-all-start = ((bf16[4,160,1408]{2,1,0:T(8,128)(2,1)}), bf16[4,160,1408]{2,1,0:T(8,128)(2,1)S(1)}, u32[]{:S(2)}, u32[]{:S(2)}) async-start(bf16[4,160,1408]{2,1,0:T(8,128)(2,1)} %copy.267), calls=%async_computation | async-start | bytes 3604480 | tf_op jit(solution)/shard_map/all_to_all | solution.py:165
  22.5 9.7 %collective-permute-done = bf16[320,1536]{1,0:T(8,128)(2,1)} collective-permute-done((bf16[320,1536]{1,0:T(8,128)(2,1)}, bf16[320,1536]{1,0:T(8,128)(2,1)}, u32[]{:S(2)}, u32[]{:S(2)}) %collective-permute-start) | collective-permute-done | bytes 983072 | tf_op jit(solution)/shard_map/ppermute | solution.py:20
  32.3 3.4 maximum_select_fusion.15
  37.6 23.0 %collective-permute-done.2 = bf16[320,1536]{1,0:T(8,128)(2,1)} collective-permute-done((bf16[320,1536]{1,0:T(8,128)(2,1)}, bf16[320,1536]{1,0:T(8,128)(2,1)}, u32[]{:S(2)}, u32[]{:S(2)}) %collective-permute-start.2) | collective-permute-done | bytes 983072 | tf_op jit(solution)/shard_map/ppermute | solution.py:20
  60.6 4.0 maximum_select_fusion.16
  64.6 15.2 %collective-permute-done.4 = bf16[320,1536]{1,0:T(8,128)(2,1)S(1)} collective-permute-done((bf16[320,1536]{1,0:T(8,128)(2,1)}, bf16[320,1536]{1,0:T(8,128)(2,1)S(1)}, u32[]{:S(2)}, u32[]{:S(2)}) %collective-permute-start.4) | collective-permute-done | bytes 983072 | tf_op jit(solution)/shard_map/ppermute | solution.py:20
  79.8 3.4 maximum_select_fusion.17
  86.5 4.9 %fusion.28 = bf16[640,1536]{1,0:T(8,128)(2,1)S(1)} fusion(bf16[640,1280]{1,0:T(8,128)(2,1)S(1)} %fusion.25, bf16[640,1536]{1,0:T(8,128)(2,1)} %collective-permute-done.1, bf16[640,1536]{1,0:T(8,128)(2,1)S(1)} %copy-done.5, pred[]{:T(512)S(6)} %eq.50), kind=kOutput, calls=%fused_computation.49 | convolution fusion | flops 2535260160 | bytes 7536641 | tf_op jit(solution)/shard_map/dot_general | solution.py:173
  93.0 6.1 %fusion.27 = bf16[640,1536]{1,0:T(8,128)(2,1)S(1)} fusion(bf16[640,1280]{1,0:T(8,128)(2,1)S(1)} %fusion.25, bf16[640,1536]{1,0:T(8,128)(2,1)} %collective-permute-done.3, bf16[640,1536]{1,0:T(8,128)(2,1)} %maximum_select_fusion.16, pred[]{:T(512)S(6)} %eq.50), kind=kOutput, calls=%fused_computation.48 | convolution fusion | flops 2535260160 | bytes 7536641 | tf_op jit(solution)/shard_map/dot_general | solution.py:173
  99.3 6.2 %fusion.26 = bf16[640,1536]{1,0:T(8,128)(2,1)S(1)} fusion(bf16[640,1280]{1,0:T(8,128)(2,1)S(1)} %fusion.25, bf16[640,1536]{1,0:T(8,128)(2,1)} %collective-permute-done.5, bf16[640,1536]{1,0:T(8,128)(2,1)} %maximum_select_fusion.17, pred[]{:T(512)S(6)} %eq.50), kind=kOutput, calls=%fused_computation.47 | convolution fusion | flops 2535260160 | bytes 7536641 | tf_op jit(solution)/shard_map/dot_general | solution.py:173
  105.7 2.2 pad_maximum_fusion
  107.9 5.0 %all-to-all-start.1 = ((bf16[4,640,384]{2,1,0:T(8,128)(2,1)}), bf16[4,640,384]{2,1,0:T(8,128)(2,1)S(1)}, u32[]{:S(2)}, u32[]{:S(2)}) async-start(bf16[4,640,384]{2,1,0:T(8,128)(2,1)} %bitcast.148), calls=%async_computation.2 | async-start | bytes 3932160 | tf_op jit(solution)/shard_map/all_to_all | solution.py:108
  116.8 3.9 constant_dynamic-slice_fusion.2
  120.7 2.7 copy.339
  128.2 83.1 %all-to-all-done.1 = bf16[4,640,384]{2,1,0:T(8,128)(2,1)S(1)} async-done(((bf16[4,640,384]{2,1,0:T(8,128)(2,1)}), bf16[4,640,384]{2,1,0:T(8,128)(2,1)S(1)}, u32[]{:S(2)}, u32[]{:S(2)}) %all-to-all-start.1) | async-done | bytes 1966112 | tf_op jit(solution)/shard_map/all_to_all | solution.py:108
  215.1 4.0 maximum_select_fusion.18
  219.1 3.9 maximum_select_fusion.19
  227.1 3.0 convert_reduce_fusion.2
  230.1 2.9 convert_reduce_fusion.3
  233.1 6.2 %collective-permute-done.6 = bf16[640,384]{1,0:T(8,128)(2,1)S(1)} collective-permute-done((bf16[640,384]{1,0:T(8,128)(2,1)S(1)}, bf16[640,384]{1,0:T(8,128)(2,1)S(1)}, u32[]{:S(2)}, u32[]{:S(2)}) %collective-permute-start.6) | collective-permute-done | bytes 491552 | tf_op jit(solution)/shard_map/ppermute | solution.py:20
  240.2 2.5 fusion.54
  243.1 19.7 %all_gather.14 = bf16[4,320,384]{2,1,0:T(8,128)(2,1)S(1)} all-gather(bf16[1,320,384]{2,1,0:T(8,128)(2,1)S(1)} %copy.302), channel_id=1, replica_groups=mesh['cfg'=2,'z'=4,'t'=2,'wt'=2] {'z'}, dimensions={0}, use_global_device_ids=true | all-gather | bytes 1228800 | tf_op jit(solution)/shard_map/all_gather | solution.py:102
  262.9 4.4 convolution_convert_fusion.2
  270.2 19.7 %all_gather.12 = bf16[4,320,384]{2,1,0:T(8,128)(2,1)S(1)} all-gather(bf16[1,320,384]{2,1,0:T(8,128)(2,1)S(1)} %copy.286), channel_id=1, replica_groups=mesh['cfg'=2,'z'=4,'t'=2,'wt'=2] {'z'}, dimensions={0}, use_global_device_ids=true | all-gather | bytes 1228800 | tf_op jit(solution)/shard_map/all_gather | solution.py:102
  290.0 5.3 %convolution_convert_fusion.5 = bf16[320,1280]{1,0:T(8,128)(2,1)} fusion(bf16[320,1536]{1,0:T(8,128)(2,1)S(1)} %bitcast.197, bf16[640,1536]{1,0:T(8,128)(2,1)} %collective-permute-done.9, bf16[640,1536]{1,0:T(8,128)(2,1)} %maximum_select_fusion.18, pred[]{:T(512)S(6)} %eq.50), kind=kOutput, calls=%fused_computation.57 | convolution fusion | flops 1276395520 | bytes 5734401 | tf_op jit(solution)/shard_map/dot_general | solution.py:219
  297.8 4.6 convolution_reduce_fusion
  302.5 7.7 %collective-permute-done.10 = bf16[320,1280]{1,0:T(8,128)(2,1)} collective-permute-done((bf16[320,1280]{1,0:T(8,128)(2,1)}, bf16[320,1280]{1,0:T(8,128)(2,1)}, u32[]{:S(2)}, u32[]{:S(2)}) %collective-permute-start.10) | collective-permute-done | bytes 819232 | tf_op jit(solution)/shard_map/ppermute | solution.py:20
  310.1 3.8 fusion.120
  314.0 5.0 %convolution_convert_fusion.1 = bf16[320,1536]{1,0:T(8,128)(2,1)S(1)} fusion(f32[320,1280]{1,0:T(8,128)S(1)} %get-tuple-element.53, bf16[640,1536]{1,0:T(8,128)(2,1)} %collective-permute-done.12, bf16[640,1536]{1,0:T(8,128)(2,1)} %maximum_select_fusion.19, pred[]{:T(512)S(6)} %eq.50), kind=kOutput, calls=%fused_computation.53 | convolution fusion | flops 1276887040 | bytes 6553601 | tf_op jit(solution)/shard_map/dot_general | solution.py:242
  320.5 4.3 all-to-all-start.3
  326.7 3.9 maximum_select_fusion.20
  330.6 5.0 %convolution_convert_fusion.4 = bf16[320,1536]{1,0:T(8,128)(2,1)S(1)} fusion(f32[320,1280]{1,0:T(8,128)S(1)} %get-tuple-element.45, bf16[640,1536]{1,0:T(8,128)(2,1)} %collective-permute-done.12, bf16[640,1536]{1,0:T(8,128)(2,1)} %maximum_select_fusion.19, pred[]{:T(512)S(6)} %eq.50), kind=kOutput, calls=%fused_computation.56 | convolution fusion | flops 1276887040 | bytes 6553601 | tf_op jit(solution)/shard_map/dot_general | solution.py:242
  336.9 7.2 %all-to-all-done.3 = bf16[4,336,384]{2,1,0:T(8,128)(2,1)} async-done(((bf16[4,336,384]{2,1,0:T(8,128)(2,1)}), bf16[4,336,384]{2,1,0:T(8,128)(2,1)}, u32[]{:S(2)}, u32[]{:S(2)}) %all-to-all-start.3) | async-done | bytes 1032224 | tf_op jit(solution)/shard_map/all_to_all | solution.py:108
  344.0 4.7 all-to-all-start.2
  351.1 2.1 copy.308
  354.4 4.5 convert_reduce_fusion
  362.2 25.6 %all_gather.15 = bf16[4,320,384]{2,1,0:T(8,128)(2,1)S(1)} all-gather(bf16[1,320,384]{2,1,0:T(8,128)(2,1)S(1)} %copy.313), channel_id=1, replica_groups=mesh['cfg'=2,'z'=4,'t'=2,'wt'=2] {'z'}, dimensions={0}, use_global_device_ids=true | all-gather | bytes 1228800 | tf_op jit(solution)/shard_map/all_gather | solution.py:102
  390.3 6.0 %convolution_convert_fusion = bf16[320,1280]{1,0:T(8,128)(2,1)} fusion(bf16[320,1536]{1,0:T(8,128)(2,1)} %bitcast.194, bf16[640,1536]{1,0:T(8,128)(2,1)} %collective-permute-done.14, bf16[640,1536]{1,0:T(8,128)(2,1)} %maximum_select_fusion.20, pred[]{:T(512)S(6)} %eq.50), kind=kOutput, calls=%fused_computation.52 | convolution fusion | flops 1276395520 | bytes 5734401 | tf_op jit(solution)/shard_map/dot_general | solution.py:219
  401.0 4.5 convert_reduce_fusion.1
  408.8 19.8 %all_gather.13 = bf16[4,320,384]{2,1,0:T(8,128)(2,1)S(1)} all-gather(bf16[1,320,384]{2,1,0:T(8,128)(2,1)S(1)} %copy.298), channel_id=1, replica_groups=mesh['cfg'=2,'z'=4,'t'=2,'wt'=2] {'z'}, dimensions={0}, use_global_device_ids=true | all-gather | bytes 1228800 | tf_op jit(solution)/shard_map/all_gather | solution.py:102
  428.7 5.4 %convolution_convert_fusion.3 = bf16[320,1280]{1,0:T(8,128)(2,1)} fusion(bf16[320,1536]{1,0:T(8,128)(2,1)S(1)} %bitcast.198, bf16[640,1536]{1,0:T(8,128)(2,1)} %collective-permute-done.14, bf16[640,1536]{1,0:T(8,128)(2,1)} %maximum_select_fusion.20, pred[]{:T(512)S(6)} %eq.50), kind=kOutput, calls=%fused_computation.55 | convolution fusion | flops 1276395520 | bytes 5734401 | tf_op jit(solution)/shard_map/dot_general | solution.py:219
  435.6 2.6 reshape.703
  438.2 2.9 dynamic-slice_reduce_fusion
  442.1 2.5 fusion.125
  444.6 4.4 collective-permute-done.15
  454.7 3.5 all-to-all-start.4
  459.9 20.1 %all-to-all-done.4 = bf16[4,160,896]{2,1,0:T(8,128)(2,1)S(1)} async-done(((bf16[4,160,896]{2,1,0:T(8,128)(2,1)}), bf16[4,160,896]{2,1,0:T(8,128)(2,1)S(1)}, u32[]{:S(2)}, u32[]{:S(2)}) %all-to-all-start.4) | async-done | bytes 1146912 | tf_op jit(solution)/shard_map/all_to_all | solution.py:299
  (232 shorter events, 71.3 us)
Async XLA Ops:
  7.2 4.8 copy-start.1
  7.2 25.1 %collective-permute-start = (bf16[320,1536]{1,0:T(8,128)(2,1)}, bf16[320,1536]{1,0:T(8,128)(2,1)}, u32[]{:S(2)}, u32[]{:S(2)}) collective-permute-start(bf16[320,1536]{1,0:T(8,128)(2,1)} %param.27), channel_id=1, source_target_pairs={{0,2},{2,0},{1,3},{3,1},{4,6},{6,4},{5,7},{7,5},{8,10},{10,8},{9,1... | collective-permute-start | bytes 2949128 | tf_op jit(solution)/shard_map/ppermute | solution.py:20
  11.9 1.9 copy-start.22
  17.0 15.3 %copy-start.8 = (bf16[320,1536]{1,0:T(8,128)(2,1)S(1)}, bf16[320,1536]{1,0:T(8,128)(2,1)}, u32[]{:S(2)}) copy-start(bf16[320,1536]{1,0:T(8,128)(2,1)} %param.27) | copy-start | bytes 2949124
  17.0 66.2 %all-to-all-start = ((bf16[4,160,1408]{2,1,0:T(8,128)(2,1)}), bf16[4,160,1408]{2,1,0:T(8,128)(2,1)S(1)}, u32[]{:S(2)}, u32[]{:S(2)}) async-start(bf16[4,160,1408]{2,1,0:T(8,128)(2,1)} %copy.267), calls=%async_computation | async-start | bytes 3604480 | tf_op jit(solution)/shard_map/all_to_all | solution.py:165
  22.0 201.8 %reduce-scatter.2.cloned.1.call-start = ((), (), s32[]{:S(2)}) async-start(), calls=%async_computation.6 | async-start | bytes 4915200 | tf_op jit(solution)/shard_map/reduce_scatter | solution.py:113
  35.6 25.0 %collective-permute-start.2 = (bf16[320,1536]{1,0:T(8,128)(2,1)}, bf16[320,1536]{1,0:T(8,128)(2,1)}, u32[]{:S(2)}, u32[]{:S(2)}) collective-permute-start(bf16[320,1536]{1,0:T(8,128)(2,1)} %param.26), channel_id=1, source_target_pairs={{0,2},{2,0},{1,3},{3,1},{4,6},{6,4},{5,7},{7,5},{8,10},{10,8},{9,1... | collective-permute-start | bytes 2949128 | tf_op jit(solution)/shard_map/ppermute | solution.py:20
  37.3 42.5 %collective-permute-start.4 = (bf16[320,1536]{1,0:T(8,128)(2,1)}, bf16[320,1536]{1,0:T(8,128)(2,1)S(1)}, u32[]{:S(2)}, u32[]{:S(2)}) collective-permute-start(bf16[320,1536]{1,0:T(8,128)(2,1)} %param.28), channel_id=1, source_target_pairs={{0,2},{2,0},{1,3},{3,1},{4,6},{6,4},{5,7},{7,5},{8,10},{10,8},{9,1... | collective-permute-start | bytes 2949128 | tf_op jit(solution)/shard_map/ppermute | solution.py:20
  37.6 47.9 %collective-permute-start.1 = (bf16[640,1536]{1,0:T(8,128)(2,1)}, bf16[640,1536]{1,0:T(8,128)(2,1)}, u32[]{:S(2)}, u32[]{:S(2)}) collective-permute-start(bf16[640,1536]{1,0:T(8,128)(2,1)} %maximum_select_fusion.15), channel_id=1, source_target_pairs={{0,16},{16,0},{1,17},{17,1},{2,18},{18,2},{3,19},{19,3},{4,20},{20... | collective-permute-start | bytes 5898248 | tf_op jit(solution)/shard_map/ppermute | solution.py:20
  64.6 28.4 %collective-permute-start.3 = (bf16[640,1536]{1,0:T(8,128)(2,1)}, bf16[640,1536]{1,0:T(8,128)(2,1)}, u32[]{:S(2)}, u32[]{:S(2)}) collective-permute-start(bf16[640,1536]{1,0:T(8,128)(2,1)} %maximum_select_fusion.16), channel_id=1, source_target_pairs={{0,16},{16,0},{1,17},{17,1},{2,18},{18,2},{3,19},{19,3},{4,20},{20... | collective-permute-start | bytes 5898248 | tf_op jit(solution)/shard_map/ppermute | solution.py:20
  83.2 16.1 %collective-permute-start.5 = (bf16[640,1536]{1,0:T(8,128)(2,1)}, bf16[640,1536]{1,0:T(8,128)(2,1)}, u32[]{:S(2)}, u32[]{:S(2)}) collective-permute-start(bf16[640,1536]{1,0:T(8,128)(2,1)} %maximum_select_fusion.17), channel_id=1, source_target_pairs={{0,16},{16,0},{1,17},{17,1},{2,18},{18,2},{3,19},{19,3},{4,20},{20... | collective-permute-start | bytes 5898248 | tf_op jit(solution)/shard_map/ppermute | solution.py:20
  83.7 1.8 copy-start
  84.8 1.6 copy-start.5
  107.9 8.8 %copy-start.27 = (s32[4]{0:T(128)S(1)}, s32[4]{0:T(128)}, u32[]{:S(2)}) copy-start(s32[4]{0:T(128)} %param.22) | copy-start | bytes 52
  107.9 103.4 %all-to-all-start.1 = ((bf16[4,640,384]{2,1,0:T(8,128)(2,1)}), bf16[4,640,384]{2,1,0:T(8,128)(2,1)S(1)}, u32[]{:S(2)}, u32[]{:S(2)}) async-start(bf16[4,640,384]{2,1,0:T(8,128)(2,1)} %bitcast.148), calls=%async_computation.2 | async-start | bytes 3932160 | tf_op jit(solution)/shard_map/all_to_all | solution.py:108
  112.9 102.2 %collective-permute-start.8 = (bf16[320,1536]{1,0:T(8,128)(2,1)}, bf16[320,1536]{1,0:T(8,128)(2,1)}, u32[]{:S(2)}, u32[]{:S(2)}) collective-permute-start(bf16[320,1536]{1,0:T(8,128)(2,1)} %param.29), channel_id=1, source_target_pairs={{0,2},{2,0},{1,3},{3,1},{4,6},{6,4},{5,7},{7,5},{8,10},{10,8},{9,1... | collective-permute-start | bytes 2949128 | tf_op jit(solution)/shard_map/ppermute | solution.py:20
  114.4 104.7 %collective-permute-start.11 = (bf16[320,1536]{1,0:T(8,128)(2,1)}, bf16[320,1536]{1,0:T(8,128)(2,1)}, u32[]{:S(2)}, u32[]{:S(2)}) collective-permute-start(bf16[320,1536]{1,0:T(8,128)(2,1)} %param.30), channel_id=1, source_target_pairs={{0,2},{2,0},{1,3},{3,1},{4,6},{6,4},{5,7},{7,5},{8,10},{10,8},{9,1... | collective-permute-start | bytes 2949128 | tf_op jit(solution)/shard_map/ppermute | solution.py:20
  114.9 211.8 %collective-permute-start.13 = (bf16[320,1536]{1,0:T(8,128)(2,1)}, bf16[320,1536]{1,0:T(8,128)(2,1)}, u32[]{:S(2)}, u32[]{:S(2)}) collective-permute-start(bf16[320,1536]{1,0:T(8,128)(2,1)} %param.31), channel_id=1, source_target_pairs={{0,2},{2,0},{1,3},{3,1},{4,6},{6,4},{5,7},{7,5},{8,10},{10,8},{9,1... | collective-permute-start | bytes 2949128 | tf_op jit(solution)/shard_map/ppermute | solution.py:20
  120.7 6.1 %copy-start.26 = (s32[1,4]{1,0:T(1,128)S(1)}, s32[1,4]{1,0:T(1,128)}, u32[]{:S(2)}) copy-start(s32[1,4]{1,0:T(1,128)} %param.25) | copy-start | bytes 52
  120.7 6.2 %copy-start.23 = (f32[128]{0:T(128)S(1)}, f32[128]{0:T(128)}, u32[]{:S(2)}) copy-start(f32[128]{0:T(128)} %constant.139) | copy-start | bytes 1540
  120.7 6.2 %copy-start.24 = (f32[128]{0:T(128)S(1)}, f32[128]{0:T(128)}, u32[]{:S(2)}) copy-start(f32[128]{0:T(128)} %constant.140) | copy-start | bytes 1540
  120.7 6.2 %copy-start.25 = (f32[128]{0:T(128)S(1)}, f32[128]{0:T(128)}, u32[]{:S(2)}) copy-start(f32[128]{0:T(128)} %constant.141) | copy-start | bytes 1540
  128.1 84.7 %copy-start.12 = (bf16[128,128,1]{1,0,2:T(8,128)(2,1)S(1)}, bf16[128,128,1]{1,0,2:T(8,128)(2,1)}, u32[]{:S(2)}) copy-start(bf16[128,128,1]{1,0,2:T(8,128)(2,1)} %constant.142) | copy-start | bytes 98308
  213.5 10.0 %collective-permute-start.7 = (bf16[640,384]{0,1:T(8,128)(2,1)S(1)}, bf16[640,384]{0,1:T(8,128)(2,1)S(1)}, u32[]{:S(2)}, u32[]{:S(2)}) collective-permute-start(bf16[640,384]{0,1:T(8,128)(2,1)S(1)} %bitcast.201), channel_id=1, source_target_pairs={{0,2},{2,0},{1,3},{3,1},{4,6},{6,4},{5,7},{7,5},{8,10},{10,8},{9,1... | collective-permute-start | bytes 1474568 | tf_op jit(solution)/shard_map/ppermute | solution.py:20
  219.1 43.8 %collective-permute-start.9 = (bf16[640,1536]{1,0:T(8,128)(2,1)}, bf16[640,1536]{1,0:T(8,128)(2,1)}, u32[]{:S(2)}, u32[]{:S(2)}) collective-permute-start(bf16[640,1536]{1,0:T(8,128)(2,1)} %maximum_select_fusion.18), channel_id=1, source_target_pairs={{0,16},{16,0},{1,17},{17,1},{2,18},{18,2},{3,19},{19,3},{4,20},{20... | collective-permute-start | bytes 5898248 | tf_op jit(solution)/shard_map/ppermute | solution.py:20
  223.0 74.8 %collective-permute-start.12 = (bf16[640,1536]{1,0:T(8,128)(2,1)}, bf16[640,1536]{1,0:T(8,128)(2,1)}, u32[]{:S(2)}, u32[]{:S(2)}) collective-permute-start(bf16[640,1536]{1,0:T(8,128)(2,1)} %maximum_select_fusion.19), channel_id=1, source_target_pairs={{0,16},{16,0},{1,17},{17,1},{2,18},{18,2},{3,19},{19,3},{4,20},{20... | collective-permute-start | bytes 5898248 | tf_op jit(solution)/shard_map/ppermute | solution.py:20
  226.0 13.2 %collective-permute-start.6 = (bf16[640,384]{1,0:T(8,128)(2,1)S(1)}, bf16[640,384]{1,0:T(8,128)(2,1)S(1)}, u32[]{:S(2)}, u32[]{:S(2)}) collective-permute-start(bf16[640,384]{1,0:T(8,128)(2,1)S(1)} %get-tuple-element.57), channel_id=1, source_target_pairs={{0,2},{2,0},{1,3},{3,1},{4,6},{6,4},{5,7},{7,5},{8,10},{10,8},{9,1... | collective-permute-start | bytes 1474568 | tf_op jit(solution)/shard_map/ppermute | solution.py:20
  227.1 3.0 copy-start.10
  262.9 6.1 %copy-start.28 = (bf16[3,320,1280]{2,1,0:T(8,128)(2,1)S(1)}, bf16[3,320,1280]{2,1,0:T(8,128)(2,1)}, u32[]{:S(2)}) copy-start(bf16[3,320,1280]{2,1,0:T(8,128)(2,1)} %get-tuple-element.92) | copy-start | bytes 7372804
  267.3 2.4 copy-start.9
  267.4 35.1 %collective-permute-start.16 = (bf16[320,1280]{1,0:T(8,128)(2,1)S(1)}, bf16[320,1280]{1,0:T(8,128)(2,1)}, u32[]{:S(2)}, u32[]{:S(2)}) collective-permute-start(bf16[320,1280]{1,0:T(8,128)(2,1)S(1)} %convolution_convert_fusion.2), channel_id=1, source_target_pairs={{0,1},{1,0},{2,3},{3,2},{4,5},{5,4},{6,7},{7,6},{8,9},{9,8},{10,11... | collective-permute-start | bytes 2457608 | tf_op jit(solution)/shard_map/ppermute | solution.py:20
  290.0 5.8 %copy-start.2 = (bf16[1,1,2048,384]{3,2,1,0:T(8,128)(2,1)S(1)}, bf16[1,1,2048,384]{3,2,1,0:T(8,128)(2,1)}, u32[]{:S(2)}) copy-start(bf16[1,1,2048,384]{3,2,1,0:T(8,128)(2,1)} %get-tuple-element.50) | copy-start | bytes 4718596
  295.3 14.8 %collective-permute-start.10 = (bf16[320,1280]{1,0:T(8,128)(2,1)}, bf16[320,1280]{1,0:T(8,128)(2,1)}, u32[]{:S(2)}, u32[]{:S(2)}) collective-permute-start(bf16[320,1280]{1,0:T(8,128)(2,1)} %convolution_convert_fusion.5), channel_id=1, source_target_pairs={{0,1},{1,0},{2,3},{3,2},{4,5},{5,4},{6,7},{7,6},{8,9},{9,8},{10,11... | collective-permute-start | bytes 2457608 | tf_op jit(solution)/shard_map/ppermute | solution.py:20
  297.8 12.4 %copy-start.18 = (f32[320]{0:T(512)}, f32[320]{0:T(512)S(1)}, u32[]{:S(2)}) copy-start(f32[320]{0:T(512)S(1)} %get-tuple-element.28) | copy-start | bytes 3844
  297.8 12.4 %copy-start.20 = (f32[320]{0:T(512)}, f32[320]{0:T(512)S(1)}, u32[]{:S(2)}) copy-start(f32[320]{0:T(512)S(1)} %get-tuple-element.29) | copy-start | bytes 3844
  319.2 5.5 %copy-start.15 = (s32[320]{0:T(512)S(1)}, s32[320]{0:T(512)}, u32[]{:S(2)}) copy-start(s32[320]{0:T(512)} %copy-done.14) | copy-start | bytes 3844
  319.2 5.5 %copy-start.17 = (s32[320]{0:T(512)S(1)}, s32[320]{0:T(512)}, u32[]{:S(2)}) copy-start(s32[320]{0:T(512)} %copy-done.16) | copy-start | bytes 3844
  320.5 23.6 %all-to-all-start.3 = ((bf16[4,336,384]{2,1,0:T(8,128)(2,1)}), bf16[4,336,384]{2,1,0:T(8,128)(2,1)}, u32[]{:S(2)}, u32[]{:S(2)}) async-start(bf16[4,336,384]{2,1,0:T(8,128)(2,1)} %fusion.61), calls=%async_computation.4 | async-start | bytes 2064384 | tf_op jit(solution)/shard_map/all_to_all | solution.py:108
  330.6 59.7 %collective-permute-start.14 = (bf16[640,1536]{1,0:T(8,128)(2,1)}, bf16[640,1536]{1,0:T(8,128)(2,1)}, u32[]{:S(2)}, u32[]{:S(2)}) collective-permute-start(bf16[640,1536]{1,0:T(8,128)(2,1)} %maximum_select_fusion.20), channel_id=1, source_target_pairs={{0,16},{16,0},{1,17},{17,1},{2,18},{18,2},{3,19},{19,3},{4,20},{20... | collective-permute-start | bytes 5898248 | tf_op jit(solution)/shard_map/ppermute | solution.py:20
  344.0 44.8 %all-to-all-start.2 = ((bf16[4,336,384]{2,1,0:T(8,128)(2,1)}), bf16[4,336,384]{2,1,0:T(8,128)(2,1)}, u32[]{:S(2)}, u32[]{:S(2)}) async-start(bf16[4,336,384]{2,1,0:T(8,128)(2,1)} %fusion.60), calls=%async_computation.3 | async-start | bytes 2064384 | tf_op jit(solution)/shard_map/all_to_all | solution.py:108
  354.4 4.5 copy-start.6
  396.3 45.8 %collective-permute-start.17 = (bf16[320,1280]{1,0:T(8,128)(2,1)}, bf16[320,1280]{1,0:T(8,128)(2,1)}, u32[]{:S(2)}, u32[]{:S(2)}) collective-permute-start(bf16[320,1280]{1,0:T(8,128)(2,1)} %convolution_convert_fusion), channel_id=1, source_target_pairs={{0,1},{1,0},{2,3},{3,2},{4,5},{5,4},{6,7},{7,6},{8,9},{9,8},{10,11... | collective-permute-start | bytes 2457608 | tf_op jit(solution)/shard_map/ppermute | solution.py:20
  401.0 4.5 copy-start.7
  434.2 14.8 %collective-permute-start.15 = (bf16[320,1280]{1,0:T(8,128)(2,1)}, bf16[320,1280]{1,0:T(8,128)(2,1)}, u32[]{:S(2)}, u32[]{:S(2)}) collective-permute-start(bf16[320,1280]{1,0:T(8,128)(2,1)} %convolution_convert_fusion.3), channel_id=1, source_target_pairs={{0,1},{1,0},{2,3},{3,2},{4,5},{5,4},{6,7},{7,6},{8,9},{9,8},{10,11... | collective-permute-start | bytes 2457608 | tf_op jit(solution)/shard_map/ppermute | solution.py:20
  453.4 4.8 copy-start.13
  453.5 6.2 %copy-start.4 = (bf16[5120,64]{0,1:T(8,128)(2,1)S(1)}, bf16[5120,64]{0,1:T(8,128)(2,1)}, u32[]{:S(2)}) copy-start(bf16[5120,64]{0,1:T(8,128)(2,1)} %param.32) | copy-start | bytes 1966084
  454.7 25.2 %all-to-all-start.4 = ((bf16[4,160,896]{2,1,0:T(8,128)(2,1)}), bf16[4,160,896]{2,1,0:T(8,128)(2,1)S(1)}, u32[]{:S(2)}, u32[]{:S(2)}) async-start(bf16[4,160,896]{2,1,0:T(8,128)(2,1)} %fusion.59), calls=%async_computation.5 | async-start | bytes 2293760 | tf_op jit(solution)/shard_map/all_to_all | solution.py:299
  480.5 1.8 collective-permute-start.18
  (6 other events, 6.9 us)
Sparse Core Ops, SparseCore 0:
  108.0 109.4 reduce-scatter.1
